TPU v7x, 256 devices: a whole 4x4x8 slice. The times are simulated.
256 devices in a mesh: seq: 128 (over z, x, y_hi, core), dp: 2 (over y_lo).
Axes of the slice: x: 4, y: 4 (y_hi: 2, y_lo: 2; y = y_hi * 2 + y_lo), z: 8, core: 2. Of those that a mesh axis runs over, the one named last changes fastest.
Arguments:
- features: bfloat16 [2, 32768, 2048], P('dp', 'seq'), may hold values from -24 to 24
- queries: bfloat16 [2, 32768, 1024], P('dp', 'seq'), may hold values from -136 to 136
- kv_weight: bfloat16 [2048, 2048], P('dp'), may hold values from -0.125 to 0.125
- upstream: bfloat16 [2, 32768, 1024], P('dp', 'seq'), may hold values from -6 to 6
Outputs:
- attended: bfloat16 [2, 32768, 1024], P('dp', 'seq')
- query_grad: bfloat16 [2, 32768, 1024], P('dp', 'seq')
- feature_grad: bfloat16 [2, 32768, 2048], P('dp', 'seq')
- weight_grad: float32 [2048, 2048], P(('dp', 'seq'))
All inputs are finite; a program needn't handle non-finite values.
Results may differ from a plain program's by a relative error of at most 0.013.
The roundings to bfloat16 on the way count: a program that leaves them out, or rounds other values in their place, can miss the bound.
Values may be sent and summed in bfloat16 or wider, within the bound.
A program may use at most 128 MiB of HBM per device.

v0:
```python
import math

import jax
import jax.numpy as jnp
from jax import lax
from jax.sharding import PartitionSpec as P

HEAD_DIM = 128
WINDOW = 2048


def passed_along(value, axis, steps):
    count = lax.axis_size(axis)
    leading, last = (max(0, -steps), min(count, count - steps))
    return lax.ppermute(value, axis, [(source, source + steps) for source in range(leading, last)])


def local(features, queries, kv_weight, upstream):
    tokens = features[0]
    query_rows = queries[0]
    upstream_rows = upstream[0]
    tok_count = tokens.shape[0]
    head_width = query_rows.shape[1]
    head_count = head_width // HEAD_DIM
    span = WINDOW // tok_count
    key_count = (span + 1) * tok_count
    score_scale = 1.0 / math.sqrt(HEAD_DIM)
    transpose_dims = (((1,), (1,)), ((), ()))
    token_dims = (((0,), (0,)), ((), ()))
    full_weight = lax.all_gather(kv_weight, "dp", axis=0, tiled=True)
    own_kv = jnp.dot(tokens, full_weight, preferred_element_type=jnp.float32).astype(jnp.bfloat16)
    earlier = []
    travelling = own_kv
    for distance in range(span):
        travelling = passed_along(travelling, "seq", 1)
        earlier.append(travelling)
    window_kv = jnp.concatenate(earlier[::-1] + [own_kv], axis=0)
    key_major = (
        window_kv[:, :head_width].reshape(key_count, head_count, HEAD_DIM).transpose(1, 0, 2)
    )
    value_major = (
        window_kv[:, head_width:].reshape(key_count, head_count, HEAD_DIM).transpose(1, 0, 2)
    )
    query_major = query_rows.reshape(tok_count, head_count, HEAD_DIM).transpose(1, 0, 2)
    grad_major = upstream_rows.reshape(tok_count, head_count, HEAD_DIM).transpose(1, 0, 2)
    first_pos = lax.axis_index("seq") * tok_count
    query_pos = lax.broadcasted_iota(jnp.int32, (tok_count, key_count), 0)
    key_pos = lax.broadcasted_iota(jnp.int32, (tok_count, key_count), 1) - span * tok_count
    allowed = (key_pos <= query_pos) & (key_pos > query_pos - WINDOW) & (first_pos + key_pos >= 0)

    def head_work(item):
        query_head, grad_head, key_head, value_head = item
        scores = (
            lax.dot_general(
                query_head, key_head, transpose_dims, preferred_element_type=jnp.float32
            )
            * score_scale
        )
        scores = jnp.where(allowed, scores, -1e30)
        row_max = jnp.max(scores, axis=-1, keepdims=True)
        exp_scores = jnp.exp(scores - row_max)
        probability = exp_scores / jnp.sum(exp_scores, axis=-1, keepdims=True)
        weights = probability.astype(jnp.bfloat16)
        attended_head = jnp.dot(weights, value_head, preferred_element_type=jnp.float32).astype(
            jnp.bfloat16
        )
        dprob = lax.dot_general(
            grad_head, value_head, transpose_dims, preferred_element_type=jnp.float32
        )
        centred = dprob - jnp.sum(probability * dprob, axis=-1, keepdims=True)
        dscore = (probability * centred * score_scale).astype(jnp.bfloat16)
        query_grad_head = jnp.dot(dscore, key_head, preferred_element_type=jnp.float32).astype(
            jnp.bfloat16
        )
        key_grad_head = lax.dot_general(
            dscore, query_head, token_dims, preferred_element_type=jnp.float32
        )
        value_grad_head = lax.dot_general(
            weights, grad_head, token_dims, preferred_element_type=jnp.float32
        )
        return (attended_head, query_grad_head, key_grad_head, value_grad_head)

    attended_all, query_grad_all, key_grad_all, value_grad_all = lax.map(
        head_work, (query_major, grad_major, key_major, value_major)
    )
    attended = attended_all.transpose(1, 0, 2).reshape(tok_count, head_width)
    query_grad = query_grad_all.transpose(1, 0, 2).reshape(tok_count, head_width)
    key_grad = key_grad_all.transpose(1, 0, 2).reshape(key_count, head_width)
    value_grad = value_grad_all.transpose(1, 0, 2).reshape(key_count, head_width)
    kv_grad_all = jnp.concatenate([key_grad, value_grad], axis=1)
    total = kv_grad_all[span * tok_count :]
    for distance in range(1, span + 1):
        portion = kv_grad_all[
            (span - distance) * tok_count : (span - distance + 1) * tok_count
        ].astype(jnp.bfloat16)
        arrived = passed_along(portion, "seq", -distance)
        total = total + arrived.astype(jnp.float32)
    kv_grad = total.astype(jnp.bfloat16)
    feature_sum = lax.dot_general(
        kv_grad, full_weight, transpose_dims, preferred_element_type=jnp.float32
    )
    feature_grad = feature_sum.astype(jnp.bfloat16)
    paired_cols = lax.all_to_all(tokens, "dp", split_axis=1, concat_axis=0, tiled=True)
    paired_grads = lax.all_gather(kv_grad, "dp", axis=0, tiled=True)
    weight_grad = lax.psum_scatter(
        lax.dot_general(paired_cols, paired_grads, token_dims, preferred_element_type=jnp.float32),
        "seq",
        scatter_dimension=0,
        tiled=True,
    )
    return (attended[None], query_grad[None], feature_grad[None], weight_grad)


def solution(mesh):
    return jax.shard_map(
        local,
        mesh=mesh,
        in_specs=(P("dp", "seq", None), P("dp", "seq", None), P("dp", None), P("dp", "seq", None)),
        out_specs=(
            P("dp", "seq", None),
            P("dp", "seq", None),
            P("dp", "seq", None),
            P(("dp", "seq"), None),
        ),
        check_vma=False,
    )
```

profile of v0, /device:TPU:1, one launch (start us, length us, event | category | flops | bytes accessed | tf_op | source)
XLA Modules:
  0.0 1377.6 jit_solution(3413439918058050031)
XLA Ops:
  8.0 114.8 %all-gather.3.cloned.1.call-done = bf16[2048,2048]{1,0:T(8,128)(2,1)} async-done(((bf16[1024,2048]{1,0:T(8,128)(2,1)}), bf16[2048,2048]{1,0:T(8,128)(2,1)}) %all-gather.3.cloned.1.call-update) | async-done | bytes 8388624 | tf_op jit(solution)/shard_map/all_gather | solution.py:30
  133.4 11.7 collective-permute-done
  145.1 5.9 collective-permute-start.1
  151.0 11.7 collective-permute-done.1
  162.7 5.9 collective-permute-start.2
  168.6 11.7 collective-permute-done.2
  181.3 5.9 collective-permute-start.3
  187.2 11.7 collective-permute-done.3
  199.9 5.9 collective-permute-start.4
  205.8 11.7 collective-permute-done.4
  218.5 5.9 collective-permute-start.5
  224.4 11.7 collective-permute-done.5
  237.1 5.9 collective-permute-start.6
  243.0 11.7 collective-permute-done.6
  254.7 6.2 collective-permute-start.7
  265.0 7.7 collective-permute-done.7
  284.9 6.1 slice_bitcast_fusion
  291.0 6.0 bitcast_bitcast_fusion
  297.0 116.3 %while.17 = (s32[]{:T(128)}, bf16[8,256,128]{2,1,0:T(8,128)(2,1)}, bf16[8,256,128]{2,1,0:T(8,128)(2,1)}, f32[8,2304,128]{1,2,0:T(8,128)}, f32[8,2304,128]{1,2,0:...) while((s32[]{:T(128)}, bf16[8,256,128]{2,1,0:T(8,128)(2,1)}, ...), condition=%wide.region_4.5_spmd.clone, body=%wide.region_0.4_spmd.clone.sunk | while | flops 920780032 | bytes 27557244 | solution.py:83
  413.3 9.1 fusion.40
  431.4 32.0 %collective-permute-done.10 = bf16[256,2048]{0,1:T(8,128)(2,1)S(1)} collective-permute-done((bf16[256,2048]{0,1:T(8,128)(2,1)S(1)}, bf16[256,2048]{0,1:T(8,128)(2,1)S(1)}, u32[]{:S(2)}, u32[]{:S(2)}) %collective-permute-start.10) | collective-permute-done | bytes 1048608 | tf_op jit(solution)/shard_map/ppermute | solution.py:15
  464.7 26.4 %collective-permute-done.11 = bf16[256,2048]{0,1:T(8,128)(2,1)S(1)} collective-permute-done((bf16[256,2048]{0,1:T(8,128)(2,1)S(1)}, bf16[256,2048]{0,1:T(8,128)(2,1)S(1)}, u32[]{:S(2)}, u32[]{:S(2)}) %collective-permute-start.11) | collective-permute-done | bytes 1048608 | tf_op jit(solution)/shard_map/ppermute | solution.py:15
  491.1 25.2 %collective-permute-start.8 = (bf16[256,2048]{0,1:T(8,128)(2,1)}, bf16[256,2048]{0,1:T(8,128)(2,1)S(1)}, u32[]{:S(2)}, u32[]{:S(2)}) collective-permute-start(bf16[256,2048]{0,1:T(8,128)(2,1)} %get-tuple-element.172), channel_id=1, source_target_pairs={{2,0},{4,2},{6,4},{8,6},{10,8},{12,10},{14,12},{16,14},{18,16},{20... | collective-permute-start | bytes 3145736 | tf_op jit(solution)/shard_map/ppermute | solution.py:15
  516.3 17.0 %collective-permute-done.12 = bf16[256,2048]{0,1:T(8,128)(2,1)S(1)} collective-permute-done((bf16[256,2048]{0,1:T(8,128)(2,1)S(1)}, bf16[256,2048]{0,1:T(8,128)(2,1)S(1)}, u32[]{:S(2)}, u32[]{:S(2)}) %collective-permute-start.12) | collective-permute-done | bytes 1048608 | tf_op jit(solution)/shard_map/ppermute | solution.py:15
  534.8 9.1 collective-permute-done.13
  543.8 39.7 %collective-permute-done.9 = bf16[256,2048]{0,1:T(8,128)(2,1)S(1)} collective-permute-done((bf16[256,2048]{0,1:T(8,128)(2,1)S(1)}, bf16[256,2048]{0,1:T(8,128)(2,1)S(1)}, u32[]{:S(2)}, u32[]{:S(2)}) %collective-permute-start.9) | collective-permute-done | bytes 1048608 | tf_op jit(solution)/shard_map/ppermute | solution.py:15
  587.2 25.9 %all_to_all.19 = bf16[256,2,1024]{0,2,1:T(8,128)(2,1)S(1)} all-to-all(bf16[256,2,1024]{0,2,1:T(8,128)(2,1)S(1)} %bitcast.131), channel_id=1, replica_groups=mesh['seq'=128,'dp'=2] {'dp'}, dimensions={1} | all-to-all | bytes 2097152 | tf_op jit(solution)/shard_map/all_to_all | solution.py:103
  613.7 75.9 %all-gather.5.cloned.1.call-done = bf16[512,2048]{0,1:T(8,128)(2,1)} async-done(((bf16[256,2048]{0,1:T(8,128)(2,1)}), bf16[512,2048]{0,1:T(8,128)(2,1)}) %all-gather.5.cloned.1.call-update) | async-done | bytes 2097168 | tf_op jit(solution)/shard_map/all_gather | solution.py:104
  689.6 7.2 convolution_bitcast_fusion.2
  696.8 9.2 copy.50
  709.7 6.7 fusion.41
  716.5 654.6 %reduce-scatter.4.cloned.1.call-done = f32[8,2048]{1,0:T(8,128)} async-done(((f32[1024,2048]{1,0:T(8,128)}), f32[8,2048]{1,0:T(8,128)}) %reduce-scatter.4.cloned.1.call-update) | async-done | bytes 65552
  (146 shorter events, 167.5 us)
Async XLA Ops:
  7.2 115.6 %copy-start.1 = (bf16[1,256,2048]{2,1,0:T(8,128)(2,1)S(1)}, bf16[1,256,2048]{2,1,0:T(8,128)(2,1)}, u32[]{:S(2)}) copy-start(bf16[1,256,2048]{2,1,0:T(8,128)(2,1)} %param.6) | copy-start | bytes 3145732
  7.2 115.6 %all-gather.3.cloned.1.call-start = ((), (), s32[]{:S(2)}) async-start(), calls=%async_computation.2 | async-start | bytes 12582912 | tf_op jit(solution)/shard_map/all_gather | solution.py:30
  7.9 681.7 %all-gather.5.cloned.1.call-start = ((), (), s32[]{:S(2)}) async-start(), calls=%async_computation.3 | async-start | bytes 3145728 | tf_op jit(solution)/shard_map/all_gather | solution.py:104
  128.5 16.6 %collective-permute-start = (bf16[256,2048]{1,0:T(8,128)(2,1)S(1)}, bf16[256,2048]{1,0:T(8,128)(2,1)S(1)}, u32[]{:S(2)}, u32[]{:S(2)}) collective-permute-start(bf16[256,2048]{1,0:T(8,128)(2,1)S(1)} %convolution_convert_fusion.3), channel_id=1, source_target_pairs={{0,2},{2,4},{4,6},{6,8},{8,10},{10,12},{12,14},{14,16},{16,18},{18... | collective-permute-start | bytes 3145736 | tf_op jit(solution)/shard_map/ppermute | solution.py:15
  145.1 17.6 %collective-permute-start.1 = (bf16[256,2048]{1,0:T(8,128)(2,1)S(1)}, bf16[256,2048]{1,0:T(8,128)(2,1)S(1)}, u32[]{:S(2)}, u32[]{:S(2)}) collective-permute-start(bf16[256,2048]{1,0:T(8,128)(2,1)S(1)} %collective-permute-done), channel_id=1, source_target_pairs={{0,2},{2,4},{4,6},{6,8},{8,10},{10,12},{12,14},{14,16},{16,18},{18... | collective-permute-start | bytes 3145736 | tf_op jit(solution)/shard_map/ppermute | solution.py:15
  162.7 17.6 %collective-permute-start.2 = (bf16[256,2048]{1,0:T(8,128)(2,1)S(1)}, bf16[256,2048]{1,0:T(8,128)(2,1)S(1)}, u32[]{:S(2)}, u32[]{:S(2)}) collective-permute-start(bf16[256,2048]{1,0:T(8,128)(2,1)S(1)} %collective-permute-done.1), channel_id=1, source_target_pairs={{0,2},{2,4},{4,6},{6,8},{8,10},{10,12},{12,14},{14,16},{16,18},{18... | collective-permute-start | bytes 3145736 | tf_op jit(solution)/shard_map/ppermute | solution.py:15
  181.3 17.6 %collective-permute-start.3 = (bf16[256,2048]{1,0:T(8,128)(2,1)S(1)}, bf16[256,2048]{1,0:T(8,128)(2,1)S(1)}, u32[]{:S(2)}, u32[]{:S(2)}) collective-permute-start(bf16[256,2048]{1,0:T(8,128)(2,1)S(1)} %collective-permute-done.2), channel_id=1, source_target_pairs={{0,2},{2,4},{4,6},{6,8},{8,10},{10,12},{12,14},{14,16},{16,18},{18... | collective-permute-start | bytes 3145736 | tf_op jit(solution)/shard_map/ppermute | solution.py:15
  199.9 17.6 %collective-permute-start.4 = (bf16[256,2048]{1,0:T(8,128)(2,1)S(1)}, bf16[256,2048]{1,0:T(8,128)(2,1)S(1)}, u32[]{:S(2)}, u32[]{:S(2)}) collective-permute-start(bf16[256,2048]{1,0:T(8,128)(2,1)S(1)} %collective-permute-done.3), channel_id=1, source_target_pairs={{0,2},{2,4},{4,6},{6,8},{8,10},{10,12},{12,14},{14,16},{16,18},{18... | collective-permute-start | bytes 3145736 | tf_op jit(solution)/shard_map/ppermute | solution.py:15
  218.5 17.6 %collective-permute-start.5 = (bf16[256,2048]{1,0:T(8,128)(2,1)S(1)}, bf16[256,2048]{1,0:T(8,128)(2,1)S(1)}, u32[]{:S(2)}, u32[]{:S(2)}) collective-permute-start(bf16[256,2048]{1,0:T(8,128)(2,1)S(1)} %collective-permute-done.4), channel_id=1, source_target_pairs={{0,2},{2,4},{4,6},{6,8},{8,10},{10,12},{12,14},{14,16},{16,18},{18... | collective-permute-start | bytes 3145736 | tf_op jit(solution)/shard_map/ppermute | solution.py:15
  237.1 17.6 %collective-permute-start.6 = (bf16[256,2048]{1,0:T(8,128)(2,1)S(1)}, bf16[256,2048]{1,0:T(8,128)(2,1)}, u32[]{:S(2)}, u32[]{:S(2)}) collective-permute-start(bf16[256,2048]{1,0:T(8,128)(2,1)S(1)} %collective-permute-done.5), channel_id=1, source_target_pairs={{0,2},{2,4},{4,6},{6,8},{8,10},{10,12},{12,14},{14,16},{16,18},{18... | collective-permute-start | bytes 3145736 | tf_op jit(solution)/shard_map/ppermute | solution.py:15
  254.7 18.0 %collective-permute-start.7 = (bf16[256,2048]{1,0:T(8,128)(2,1)}, bf16[256,2048]{1,0:T(8,128)(2,1)}, u32[]{:S(2)}, u32[]{:S(2)}) collective-permute-start(bf16[256,2048]{1,0:T(8,128)(2,1)} %collective-permute-done.6), channel_id=1, source_target_pairs={{0,2},{2,4},{4,6},{6,8},{8,10},{10,12},{12,14},{14,16},{16,18},{18... | collective-permute-start | bytes 3145736 | tf_op jit(solution)/shard_map/ppermute | solution.py:15
  265.0 12.5 copy-start.9
  275.1 3.5 copy-start.7
  277.5 2.1 copy-start.5
  278.5 2.1 copy-start.3
  413.3 170.2 %slice-start = ((s8[9437184]{0:T(1024)(128)(4,1)}), s8[4194304]{0:T(1024)(128)(4,1)S(1)}, s32[]{:S(2)}) async-start(s8[9437184]{0:T(1024)(128)(4,1)} %bitcast.123), calls=%async_computation.5 | async-start | bytes 8388608
  413.3 170.2 %slice-start.1 = ((s8[9437184]{0:T(1024)(128)(4,1)}), s8[4194304]{0:T(1024)(128)(4,1)S(1)}, s32[]{:S(2)}) async-start(s8[9437184]{0:T(1024)(128)(4,1)} %bitcast.123), calls=%async_computation.6 | async-start | bytes 8388608
  413.3 170.2 %slice-start.3 = ((s8[9437184]{0:T(1024)(128)(4,1)}), s8[4194304]{0:T(1024)(128)(4,1)S(1)}, s32[]{:S(2)}) async-start(s8[9437184]{0:T(1024)(128)(4,1)} %bitcast.127), calls=%async_computation.8 | async-start | bytes 8388608
  413.3 170.2 %slice-start.4 = ((s8[9437184]{0:T(1024)(128)(4,1)}), s8[4194304]{0:T(1024)(128)(4,1)S(1)}, s32[]{:S(2)}) async-start(s8[9437184]{0:T(1024)(128)(4,1)} %bitcast.127), calls=%async_computation.9 | async-start | bytes 8388608
  422.4 161.1 %slice-start.2 = ((s8[9437184]{0:T(1024)(128)(4,1)}), s8[1048576]{0:T(1024)(128)(4,1)S(1)}, s32[]{:S(2)}) async-start(s8[9437184]{0:T(1024)(128)(4,1)} %bitcast.123), calls=%async_computation.7 | async-start | bytes 2097152
  422.5 161.1 %slice-start.5 = ((s8[9437184]{0:T(1024)(128)(4,1)}), s8[1048576]{0:T(1024)(128)(4,1)S(1)}, s32[]{:S(2)}) async-start(s8[9437184]{0:T(1024)(128)(4,1)} %bitcast.127), calls=%async_computation.10 | async-start | bytes 2097152
  424.7 38.7 %collective-permute-start.10 = (bf16[256,2048]{0,1:T(8,128)(2,1)S(1)}, bf16[256,2048]{0,1:T(8,128)(2,1)S(1)}, u32[]{:S(2)}, u32[]{:S(2)}) collective-permute-start(bf16[256,2048]{0,1:T(8,128)(2,1)S(1)} %get-tuple-element.178), channel_id=1, source_target_pairs={{6,0},{8,2},{10,4},{12,6},{14,8},{16,10},{18,12},{20,14},{22,16},{... | collective-permute-start | bytes 3145736 | tf_op jit(solution)/shard_map/ppermute | solution.py:15
  426.2 64.8 %collective-permute-start.11 = (bf16[256,2048]{0,1:T(8,128)(2,1)S(1)}, bf16[256,2048]{0,1:T(8,128)(2,1)S(1)}, u32[]{:S(2)}, u32[]{:S(2)}) collective-permute-start(bf16[256,2048]{0,1:T(8,128)(2,1)S(1)} %get-tuple-element.177), channel_id=1, source_target_pairs={{8,0},{10,2},{12,4},{14,6},{16,8},{18,10},{20,12},{22,14},{24,16},... | collective-permute-start | bytes 3145736 | tf_op jit(solution)/shard_map/ppermute | solution.py:15
  427.5 105.7 %collective-permute-start.12 = (bf16[256,2048]{0,1:T(8,128)(2,1)S(1)}, bf16[256,2048]{0,1:T(8,128)(2,1)S(1)}, u32[]{:S(2)}, u32[]{:S(2)}) collective-permute-start(bf16[256,2048]{0,1:T(8,128)(2,1)S(1)} %get-tuple-element.176), channel_id=1, source_target_pairs={{10,0},{12,2},{14,4},{16,6},{18,8},{20,10},{22,12},{24,14},{26,16}... | collective-permute-start | bytes 3145736 | tf_op jit(solution)/shard_map/ppermute | solution.py:15
  428.8 115.0 %collective-permute-start.13 = (bf16[256,2048]{0,1:T(8,128)(2,1)}, bf16[256,2048]{0,1:T(8,128)(2,1)S(1)}, u32[]{:S(2)}, u32[]{:S(2)}) collective-permute-start(bf16[256,2048]{0,1:T(8,128)(2,1)} %get-tuple-element.175), channel_id=1, source_target_pairs={{12,0},{14,2},{16,4},{18,6},{20,8},{22,10},{24,12},{26,14},{28,16}... | collective-permute-start | bytes 3145736 | tf_op jit(solution)/shard_map/ppermute | solution.py:15
  430.1 113.7 %collective-permute-start.14 = (bf16[256,2048]{0,1:T(8,128)(2,1)}, bf16[256,2048]{0,1:T(8,128)(2,1)S(1)}, u32[]{:S(2)}, u32[]{:S(2)}) collective-permute-start(bf16[256,2048]{0,1:T(8,128)(2,1)} %get-tuple-element.174), channel_id=1, source_target_pairs={{14,0},{16,2},{18,4},{20,6},{22,8},{24,10},{26,12},{28,14},{30,16}... | collective-permute-start | bytes 3145736 | tf_op jit(solution)/shard_map/ppermute | solution.py:15
  463.4 80.4 %collective-permute-start.15 = (bf16[256,2048]{0,1:T(8,128)(2,1)}, bf16[256,2048]{0,1:T(8,128)(2,1)S(1)}, u32[]{:S(2)}, u32[]{:S(2)}) collective-permute-start(bf16[256,2048]{0,1:T(8,128)(2,1)} %get-tuple-element.173), channel_id=1, source_target_pairs={{16,0},{18,2},{20,4},{22,6},{24,8},{26,10},{28,12},{30,14},{32,16}... | collective-permute-start | bytes 3145736 | tf_op jit(solution)/shard_map/ppermute | solution.py:15
  491.1 52.8 %collective-permute-start.8 = (bf16[256,2048]{0,1:T(8,128)(2,1)}, bf16[256,2048]{0,1:T(8,128)(2,1)S(1)}, u32[]{:S(2)}, u32[]{:S(2)}) collective-permute-start(bf16[256,2048]{0,1:T(8,128)(2,1)} %get-tuple-element.172), channel_id=1, source_target_pairs={{2,0},{4,2},{6,4},{8,6},{10,8},{12,10},{14,12},{16,14},{18,16},{20... | collective-permute-start | bytes 3145736 | tf_op jit(solution)/shard_map/ppermute | solution.py:15
  533.3 50.3 %collective-permute-start.9 = (bf16[256,2048]{0,1:T(8,128)(2,1)S(1)}, bf16[256,2048]{0,1:T(8,128)(2,1)S(1)}, u32[]{:S(2)}, u32[]{:S(2)}) collective-permute-start(bf16[256,2048]{0,1:T(8,128)(2,1)S(1)} %get-tuple-element.179), channel_id=1, source_target_pairs={{4,0},{6,2},{8,4},{10,6},{12,8},{14,10},{16,12},{18,14},{20,16},{2... | collective-permute-start | bytes 3145736 | tf_op jit(solution)/shard_map/ppermute | solution.py:15
  585.7 785.3 %reduce-scatter.4.cloned.1.call-start = ((), (), s32[]{:S(2)}) async-start(), calls=%async_computation.4 | async-start | bytes 8454144
  706.0 2.4 copy-start.11
  706.0 3.7 copy-start
  (5 other events, 5.0 us)
Sparse Core Ops, SparseCore 0:
  9.8 112.8 all-gather.2
  585.8 103.7 all-gather.4
  706.1 664.8 reduce-scatter.3
where the time goes:
time: 1390 us; the launch traced here: 1380 us
  waiting for transfers between devices  1060 us (76%)
  matrix products  126 us (9%)
  starting transfers between devices  81.2 us (6%)
  local copies, waits for them, and re-layouts  49.4 us (4%)
  blocking collectives  25.9 us (2%)
  other arithmetic  21 us (2%)
  between operations  14.1 us (1%)
    unnamed x4, waiting for transfers between devices  655 us
    ppermute x16, waiting for transfers between devices, passed_along(): lax.ppermute(value, axis, [(source, source + steps) for source in range(l...  214 us
    all_gather x1, waiting for transfers between devices, local(): full_weight = lax.all_gather(kv_weight, 'dp', axis=0, tiled=True)  115 us
    ppermute x16, starting transfers between devices, passed_along(): lax.ppermute(value, axis, [(source, source + steps) for source in range(l...  81 us
    all_gather x1, waiting for transfers between devices, local(): paired_grads = lax.all_gather(kv_grad, 'dp', axis=0, tiled=True)  75.9 us
    unnamed x49, local copies, waits for them, and re-layouts  36.9 us
  transfers between devices with their start and end apart: 19, of which 16 were waited for; matrix products, arithmetic and copies ran while one was open for 1% of the time, Pallas kernels for 0%

commit v1 on v0

v1 whole, which is shorter than its diff:
```python
import math

import jax
import jax.numpy as jnp
from jax import lax
from jax.experimental import pallas as pl
from jax.experimental.pallas import tpu as pltpu
from jax.sharding import PartitionSpec as P

HD = 128
BLK = 256
SPAN = 8
NEG = -1e30
MESH = pl.DeviceIdType.MESH
BF = jnp.bfloat16
F32 = jnp.float32
SCALE = 1.0 / math.sqrt(HD)
EXP_SCALE = SCALE * math.log2(math.e)
NT = (((1,), (1,)), ((), ()))
TN = (((0,), (0,)), ((), ()))


def loop(lo, hi, body):
    def step(i, carry):
        body(i)
        return carry

    lax.fori_loop(lo, hi, step, 0)


def place():
    seq = lax.axis_index("seq")
    dp = lax.axis_index("dp")
    return seq, dp, seq % 4, seq - seq % 4


def remote(src, dst, send, recv, seq, dp):
    return pltpu.make_async_remote_copy(
        src_ref=src, dst_ref=dst, send_sem=send, recv_sem=recv,
        device_id={"seq": seq, "dp": dp}, device_id_type=MESH,
    )


def greet(partners):
    barrier = pltpu.get_barrier_semaphore()
    for seq, dp in partners:
        pl.semaphore_signal(barrier, inc=1, device_id={"seq": seq, "dp": dp}, device_id_type=MESH)
    pl.semaphore_wait(barrier, len(partners))


def attention_kernel(
    x_in, q_in, w_in, up_in,
    att_out, dq_out, fg_out, kvf_out, fall_out,
    wf, xv, stage, kbuf, kvt, qbuf, s_ref, dp_ref, dkv, sbuf, rbuf, kvf, kvg, obuf, fgv,
    wl, ws, wr, wfs, wfr, xl, ks, kr, kl, hs, hr, qs, qr, ql, fs, fr, fl,
    os_, or_, ol, rs, rr, gs, gr, gl, el,
):
    n_seq = lax.axis_size("seq")
    seq, dp, me, base = place()
    core = seq % 2
    y_hi = (seq // 2) % 2
    other = 1 - dp
    up_y = (y_hi + dp) % 2
    down_y = (y_hi + 1 - dp) % 2
    up_seq = base + up_y * 2 + core
    down_seq = base + down_y * 2 + core
    w_seq = base + ((y_hi + (1 - dp) * (1 - core) + dp * core) % 2) * 2 + core
    pair_seq = base + y_hi * 2 + (1 - core)
    near_next = (seq + 4) % n_seq
    far_next = (seq + 8) % n_seq
    near_prev = (seq + n_seq - 4) % n_seq
    far_prev = (seq + n_seq - 8) % n_seq

    def cols(head_pos, kv):
        return pl.ds(pl.multiple_of(kv * 1024 + head_pos * HD, HD), HD)

    def w_local(hl, j, kv):
        return pltpu.make_async_copy(
            w_in.at[:, cols(2 * j + hl, kv)],
            wf.at[hl * 4 + j, pl.ds(pl.multiple_of(dp * 1024, 1024), 1024), pl.ds(kv * HD, HD)],
            wl.at[hl * 4 + j, kv],
        )

    def w_rows(which_dp, which_core):
        return pl.ds(pl.multiple_of(which_dp * 1024 + which_core * 512, 512), 512)

    def w_send(hl, j, kv):
        return remote(
            w_in.at[pl.ds(pl.multiple_of(core * 512, 512), 512), cols(2 * j + hl, kv)],
            wf.at[hl * 4 + j, w_rows(dp, core), pl.ds(kv * HD, HD)],
            ws.at[hl * 4 + j, kv], wr.at[hl * 4 + j, kv], w_seq, other,
        )

    def w_arrive(hl, j, kv):
        part = wf.at[hl * 4 + j, w_rows(other, core), pl.ds(kv * HD, HD)]
        return remote(part, part, ws.at[hl * 4 + j, kv], wr.at[hl * 4 + j, kv], w_seq, other)

    def w_swap(hl, j, which_core):
        part = wf.at[hl * 4 + j, w_rows(other, which_core), :]
        return remote(part, part, wfs.at[hl * 4 + j], wfr.at[hl * 4 + j], pair_seq, dp)

    def kv_send(hl, j):
        return remote(
            stage.at[hl * 4 + j], kbuf.at[hl, SPAN + me], ks.at[hl, j], kr.at[hl, me], base + j, dp
        )

    def kv_arrive(hl, j):
        return remote(
            stage.at[hl * 4 + j], kbuf.at[hl, SPAN + j], ks.at[hl, j], kr.at[hl, j], base + j, dp
        )

    def kv_local(hl):
        return pltpu.make_async_copy(stage.at[hl * 4 + me], kbuf.at[hl, SPAN + me], kl.at[hl])

    def halo(hl, i, far):
        return remote(
            kbuf.at[hl, SPAN + i], kbuf.at[hl, (1 - far) * 4 + i],
            hs.at[hl, far, i], hr.at[hl, far, i], far_next if far else near_next, dp,
        )

    def q_copy(hl, j, which):
        src = (q_in, up_in)[which].at[:, cols(2 * j + hl, 0)]
        return src, qbuf.at[hl, me, :, pl.ds(which * HD, HD)]

    def q_send(hl, j, which):
        src, dst = q_copy(hl, j, which)
        return remote(src, dst, qs.at[hl, j, which], qr.at[hl, me, which], base + j, dp)

    def q_arrive(hl, j, which):
        src, _ = q_copy(hl, j, which)
        return remote(
            src, qbuf.at[hl, j, :, pl.ds(which * HD, HD)],
            qs.at[hl, j, which], qr.at[hl, j, which], base + j, dp,
        )

    def q_local(hl, which):
        src, dst = q_copy(hl, me, which)
        return pltpu.make_async_copy(src, dst, ql.at[hl, which])

    def x_cols(which_dp):
        return x_in.at[:, pl.ds(pl.multiple_of(which_dp * 1024, 1024), 1024)]

    def f_send(j, d):
        return remote(x_cols(d), fall_out.at[dp, me], fs.at[d, j], fr.at[dp, me], base + j, d)

    def f_arrive(j, d):
        return remote(x_cols(d), fall_out.at[d, j], fs.at[d, j], fr.at[d, j], base + j, d)

    def f_local():
        return pltpu.make_async_copy(x_cols(dp), fall_out.at[dp, me], fl)

    def o_send(hl, j, which):
        out = (att_out, dq_out)[which]
        return remote(
            obuf.at[hl, j, :, pl.ds(which * HD, HD)], out.at[:, cols(2 * me + hl, 0)],
            os_.at[hl, j, which], or_.at[hl, me, which], base + j, dp,
        )

    def o_arrive(hl, j, which):
        out = (att_out, dq_out)[which]
        return remote(
            obuf.at[hl, j, :, pl.ds(which * HD, HD)], out.at[:, cols(2 * j + hl, 0)],
            os_.at[hl, j, which], or_.at[hl, j, which], base + j, dp,
        )

    def o_local(hl, which):
        out = (att_out, dq_out)[which]
        return pltpu.make_async_copy(
            obuf.at[hl, me, :, pl.ds(which * HD, HD)], out.at[:, cols(2 * me + hl, 0)],
            ol.at[hl, which],
        )

    def back(hl, i, far):
        return remote(
            sbuf.at[hl, (1 - far) * 4 + i], rbuf.at[hl, far, i],
            rs.at[hl, far, i], rr.at[hl, far, i], far_prev if far else near_prev, dp,
        )

    def g_send(hl, j):
        return remote(
            kvf.at[hl, j], kvg.at[hl * 4 + me], gs.at[hl, j], gr.at[hl, me], base + j, dp
        )

    def g_arrive(hl, j):
        return remote(
            kvf.at[hl, j], kvg.at[hl * 4 + j], gs.at[hl, j], gr.at[hl, j], base + j, dp
        )

    def g_local(hl):
        return pltpu.make_async_copy(kvf.at[hl, me], kvg.at[hl * 4 + me], gl.at[hl])

    def others(body):
        loop(1, 4, lambda r: body((me + r) % 4))

    def project(hl):
        def forward(j):
            w_arrive(hl, j, 0).wait_recv()
            w_arrive(hl, j, 1).wait_recv()
            w_swap(hl, j, core).start()

        loop(0, 4, forward)

        def one(r):
            j = (me + r) % 4
            w_local(hl, j, 0).wait()
            w_local(hl, j, 1).wait()
            w_swap(hl, j, 1 - core).wait_recv()
            kv = jnp.dot(xv[...], wf[hl * 4 + j], preferred_element_type=F32)
            stage[hl * 4 + j] = kv.astype(BF)

            @pl.when(r < 4)
            def _():
                kv_send(hl, j).start()

            @pl.when(r == 4)
            def _():
                kv_local(hl).start()

        loop(1, 5, one)

    def send_halo(hl):
        kv_local(hl).wait()

        def go(i):
            halo(hl, i, 0).start()
            halo(hl, i, 1).start()

        go(me)

        def one(i):
            kv_arrive(hl, i).wait_recv()
            go(i)

        others(one)

    def attend(hl):
        def clear(b):
            dkv[hl, b] = jnp.zeros((BLK, 2 * HD), F32)
            kvt[b] = kbuf[hl, b].T

        loop(0, 12, clear)
        rows = lax.broadcasted_iota(jnp.int32, (BLK, BLK), 0)
        columns = lax.broadcasted_iota(jnp.int32, (BLK, BLK), 1)

        def one_block(qi):
            query = qbuf[hl, qi, :, :HD]
            grad = qbuf[hl, qi, :, HD:]
            first = base - SPAN + qi
            top = None
            for w in range(SPAN + 1):
                scores = lax.dot_general(
                    kbuf[hl, qi + w, :, :HD], query, NT, preferred_element_type=F32
                )
                if w == 0:
                    scores = jnp.where(rows > columns, scores, NEG)
                if w == SPAN:
                    scores = jnp.where(rows <= columns, scores, NEG)
                s_ref[w] = scores
                here = jnp.max(scores, axis=0, keepdims=True)
                if w < SPAN:
                    here = jnp.where(first + w >= 0, here, NEG)
                top = here if top is None else jnp.maximum(top, here)
                dp_ref[w] = lax.dot_general(
                    kbuf[hl, qi + w, :, HD:], grad, NT, preferred_element_type=F32
                )
            top = top * EXP_SCALE
            total = jnp.zeros((1, BLK), F32)
            weighted = jnp.zeros((1, BLK), F32)
            for w in range(SPAN + 1):
                shift = jnp.where(first + w >= 0, top, -NEG) if w < SPAN else top
                e = jnp.exp2(s_ref[w] * EXP_SCALE - shift)
                s_ref[w] = e
                total = total + jnp.sum(e, axis=0, keepdims=True)
                weighted = weighted + jnp.sum(e * dp_ref[w], axis=0, keepdims=True)
            inverse = 1.0 / total
            mean = weighted * inverse
            inverse_scaled = inverse * SCALE
            att = jnp.zeros((HD, BLK), F32)
            dq = jnp.zeros((HD, BLK), F32)
            for w in range(SPAN + 1):
                e = s_ref[w]
                weights = (e * inverse).astype(BF)
                dscore = ((e * inverse_scaled) * (dp_ref[w] - mean)).astype(BF)
                dkv[hl, qi + w, :, :HD] += jnp.dot(dscore, query, preferred_element_type=F32)
                dkv[hl, qi + w, :, HD:] += jnp.dot(weights, grad, preferred_element_type=F32)
                att = att + jnp.dot(kvt[qi + w, HD:, :], weights, preferred_element_type=F32)
                dq = dq + jnp.dot(kvt[qi + w, :HD, :], dscore, preferred_element_type=F32)
            obuf[hl, qi, :, :HD] = att.T.astype(BF)
            obuf[hl, qi, :, HD:] = dq.T.astype(BF)

            @pl.when(qi == me)
            def _():
                o_local(hl, 0).start()
                o_local(hl, 1).start()

            @pl.when(qi != me)
            def _():
                o_send(hl, qi, 0).start()
                o_send(hl, qi, 1).start()

            sbuf[hl, qi] = dkv[hl, qi].astype(BF)
            back(hl, qi, 1).start()

        loop(0, 4, one_block)

        def one_back(i):
            sbuf[hl, 4 + i] = dkv[hl, 4 + i].astype(BF)
            back(hl, i, 0).start()

        loop(0, 4, one_back)

    def finish(hl):
        def one(i):
            back(hl, i, 0).wait_recv()
            back(hl, i, 1).wait_recv()
            whole = dkv[hl, SPAN + i] + rbuf[hl, 0, i].astype(F32) + rbuf[hl, 1, i].astype(F32)
            kvf[hl, i] = whole.astype(BF)

            @pl.when(i == me)
            def _():
                g_local(hl).start()

            @pl.when(i != me)
            def _():
                g_send(hl, i).start()

        loop(0, 4, one)

    x_copy = pltpu.make_async_copy(x_in, xv, xl)
    x_copy.start()
    for hl in range(2):
        for kv in range(2):
            loop(0, 4, lambda j: w_local(hl, j, kv).start())
    greet(
        [(base + (me + r) % 4, dp) for r in range(4) if r]
        + [(base + (me + r) % 4, other) for r in range(4)]
        + [(near_next, dp), (far_next, dp), (near_prev, dp), (far_prev, dp)]
    )

    def w_start(hl):
        def one(j):
            w_send(hl, j, 0).start()
            w_send(hl, j, 1).start()

        loop(0, 4, one)

    def q_start(hl):
        q_local(hl, 0).start()
        q_local(hl, 1).start()

        def one(j):
            q_send(hl, j, 0).start()
            q_send(hl, j, 1).start()

        others(one)

    w_start(0)
    x_copy.wait()
    project(0)
    others(lambda j: kv_send(0, j).wait_send())
    w_start(1)
    q_start(0)
    send_halo(0)
    project(1)
    q_start(1)
    send_halo(1)
    f_local().start()
    loop(1, 8, lambda t: f_send((me + t % 4) % 4, (dp + t // 4) % 2).start())

    def ready(hl):
        def one(i):
            halo(hl, i, 0).wait_recv()
            halo(hl, i, 1).wait_recv()

        loop(0, 4, one)
        q_local(hl, 0).wait()
        q_local(hl, 1).wait()

        def two(j):
            q_arrive(hl, j, 0).wait_recv()
            q_arrive(hl, j, 1).wait_recv()

        others(two)

    ready(0)
    attend(0)
    ready(1)
    attend(1)
    finish(0)
    finish(1)
    kvf_copy = pltpu.make_async_copy(kvf, kvf_out, el.at[0])
    kvf_copy.start()
    for hl in range(2):
        g_local(hl).wait()
        others(lambda j: g_arrive(hl, j).wait_recv())

    def feature(n):
        at = pl.multiple_of(n * 256, 256)
        acc = jnp.zeros((BLK, 256), F32)
        for idx in range(8):
            acc = acc + lax.dot_general(
                kvg[idx], wf[idx, pl.ds(at, 256), :], NT, preferred_element_type=F32
            )
        fgv[:, pl.ds(at, 256)] = acc.astype(BF)

    loop(0, 8, feature)
    fg_copy = pltpu.make_async_copy(fgv, fg_out, el.at[1])
    fg_copy.start()

    for hl in range(2):
        def w_end(j):
            w_send(hl, j, 0).wait_send()
            w_send(hl, j, 1).wait_send()
            w_swap(hl, j, core).wait_send()

        loop(0, 4, w_end)

        def four_end(i):
            for far in range(2):
                halo(hl, i, far).wait_send()
                back(hl, i, far).wait_send()

        loop(0, 4, four_end)

        def three_end(j):
            if hl == 1:
                kv_send(hl, j).wait_send()
            g_send(hl, j).wait_send()
            for which in range(2):
                q_send(hl, j, which).wait_send()
                o_send(hl, j, which).wait_send()
                o_arrive(hl, j, which).wait_recv()

        others(three_end)
        o_local(hl, 0).wait()
        o_local(hl, 1).wait()
    f_local().wait()

    def f_end(t):
        j, d = (me + t % 4) % 4, (dp + t // 4) % 2
        f_send(j, d).wait_send()
        f_arrive(j, d).wait_recv()

    loop(1, 8, f_end)
    kvf_copy.wait()
    fg_copy.wait()


def weight_kernel(
    fall_in, kvf_in, dw_out,
    fv, gv, dwb, r1, dz, r2, s3, r3,
    il, ps, pr, s1s, s1r, s2s, s2r, s3s, s3r,
):
    n_z = lax.axis_size("seq") // 16
    seq, dp, me, base = place()
    xi = (seq // 4) % 4
    zi = seq // 16
    other = 1 - dp

    f_copy = pltpu.make_async_copy(fall_in, fv, il.at[0])
    g_copy = pltpu.make_async_copy(kvf_in, gv.at[dp], il.at[1])
    f_copy.start()
    g_copy.start()
    x_seq = lambda x: zi * 16 + x * 4 + me
    z_seq = lambda z: z * 16 + xi * 4 + me
    greet(
        [(seq, other)]
        + [(base + (me + r) % 4, dp) for r in range(1, 4)]
        + [(x_seq((xi + r) % 4), dp) for r in range(1, 4)]
        + [(z_seq((zi + r) % n_z), dp) for r in range(1, n_z)]
    )
    p_copy = remote(kvf_in, gv.at[dp], ps, pr, seq, other)
    p_copy.start()
    f_copy.wait()
    g_copy.wait()
    remote(kvf_in, gv.at[other], ps, pr, seq, other).wait_recv()

    def tile(t):
        at = pl.multiple_of(t * 256, 256)
        for hl in range(2):
            acc = jnp.zeros((256, 2 * HD), F32)
            for s in range(2):
                for b in range(4):
                    acc = acc + lax.dot_general(
                        fv[s, b, :, pl.ds(at, 256)], gv[s, hl, b], TN, preferred_element_type=F32
                    )
            for zz in range(2):
                for xx in range(4):
                    lo = (zz * 4 + xx) * 32
                    dwb[xx, 2 * t + zz, :, hl * 256:(hl + 1) * 256] = acc[lo:lo + 32].astype(BF)

    loop(0, 4, tile)

    def first(x):
        return remote(dwb.at[x], r1.at[xi], s1s.at[x], s1r.at[xi], x_seq(x), dp)

    def first_arrive(x):
        return remote(dwb.at[x], r1.at[x], s1s.at[x], s1r.at[x], x_seq(x), dp)

    loop(1, 4, lambda r: first((xi + r) % 4).start())
    loop(1, 4, lambda r: first_arrive((xi + r) % 4).wait_recv())

    def second(z):
        return remote(dz.at[z], r2.at[zi], s2s.at[z], s2r.at[zi], z_seq(z), dp)

    def second_arrive(z):
        return remote(dz.at[z], r2.at[z], s2s.at[z], s2r.at[z], z_seq(z), dp)

    def add_x(z):
        acc = dwb[xi, z].astype(F32)
        for r in range(1, 4):
            acc = acc + r1[(xi + r) % 4, z].astype(F32)
        return acc

    def one_z(r):
        z = (zi + r) % n_z
        dz[z] = add_x(z).astype(BF)
        second(z).start()

    loop(1, n_z, one_z)
    acc = add_x(zi)
    loop(1, n_z, lambda r: second_arrive((zi + r) % n_z).wait_recv())
    for r in range(1, n_z):
        acc = acc + r2[(zi + r) % n_z].astype(F32)
    for j in range(4):
        s3[j] = acc[j * 8:(j + 1) * 8]

    def third(j):
        return remote(s3.at[j], r3.at[me], s3s.at[j], s3r.at[me], base + j, dp)

    def third_arrive(j):
        return remote(s3.at[j], r3.at[j], s3s.at[j], s3r.at[j], base + j, dp)

    loop(1, 4, lambda r: third((me + r) % 4).start())
    r3[me] = s3[me]
    loop(1, 4, lambda r: third_arrive((me + r) % 4).wait_recv())
    for j in range(4):
        for hl in range(2):
            for kv in range(2):
                head = kv * 1024 + (2 * j + hl) * HD
                lo = hl * 256 + kv * HD
                dw_out[:, head:head + HD] = r3[j, :, lo:lo + HD]

    p_copy.wait_send()
    loop(1, 4, lambda r: first((xi + r) % 4).wait_send())
    loop(1, n_z, lambda r: second((zi + r) % n_z).wait_send())
    loop(1, 4, lambda r: third((me + r) % 4).wait_send())


def local(features, queries, kv_weight, upstream):
    dma = pltpu.SemaphoreType.DMA
    anywhere = pl.BlockSpec(memory_space=pl.ANY)
    vmem = pl.BlockSpec(memory_space=pltpu.VMEM)
    sds = jax.ShapeDtypeStruct
    att, dq, fg, kvf, fall = pl.pallas_call(
        attention_kernel,
        out_shape=(
            sds((256, 1024), BF), sds((256, 1024), BF), sds((256, 2048), BF),
            sds((2, 4, 256, 256), BF), sds((2, 4, 256, 1024), BF),
        ),
        in_specs=[anywhere] * 4,
        out_specs=(anywhere,) * 5,
        scratch_shapes=[
            pltpu.VMEM((8, 2048, 256), BF),
            pltpu.VMEM((256, 2048), BF),
            pltpu.VMEM((8, 256, 256), BF),
            pltpu.VMEM((2, 12, 256, 256), BF),
            pltpu.VMEM((12, 256, 256), BF),
            pltpu.VMEM((2, 4, 256, 256), BF),
            pltpu.VMEM((9, 256, 256), F32),
            pltpu.VMEM((9, 256, 256), F32),
            pltpu.VMEM((2, 12, 256, 256), F32),
            pltpu.VMEM((2, 8, 256, 256), BF),
            pltpu.VMEM((2, 2, 4, 256, 256), BF),
            pltpu.VMEM((2, 4, 256, 256), BF),
            pltpu.VMEM((8, 256, 256), BF),
            pltpu.VMEM((2, 4, 256, 256), BF),
            pltpu.VMEM((256, 2048), BF),
            dma((8, 2)), dma((8, 2)), dma((8, 2)), dma((8,)), dma((8,)), dma,
            dma((2, 4)), dma((2, 4)), dma((2,)),
            dma((2, 2, 4)), dma((2, 2, 4)),
            dma((2, 4, 2)), dma((2, 4, 2)), dma((2, 2)),
            dma((2, 4)), dma((2, 4)), dma,
            dma((2, 4, 2)), dma((2, 4, 2)), dma((2, 2)),
            dma((2, 2, 4)), dma((2, 2, 4)),
            dma((2, 4)), dma((2, 4)), dma((2,)), dma((2,)),
        ],
        compiler_params=pltpu.CompilerParams(
            collective_id=0, has_side_effects=True, vmem_limit_bytes=56 << 20
        ),
        name="attention",
    )(features[0], queries[0], kv_weight, upstream[0])
    weight_grad = pl.pallas_call(
        weight_kernel,
        out_shape=sds((8, 2048), F32),
        in_specs=[anywhere] * 2,
        out_specs=vmem,
        scratch_shapes=[
            pltpu.VMEM((2, 4, 256, 1024), BF),
            pltpu.VMEM((2, 2, 4, 256, 256), BF),
            pltpu.VMEM((4, 8, 32, 512), BF),
            pltpu.VMEM((4, 8, 32, 512), BF),
            pltpu.VMEM((8, 32, 512), BF),
            pltpu.VMEM((8, 32, 512), BF),
            pltpu.VMEM((4, 8, 512), F32),
            pltpu.VMEM((4, 8, 512), F32),
            dma((2,)), dma, dma,
            dma((4,)), dma((4,)), dma((8,)), dma((8,)), dma((4,)), dma((4,)),
        ],
        compiler_params=pltpu.CompilerParams(
            collective_id=1, has_side_effects=True, vmem_limit_bytes=40 << 20
        ),
        name="weight_gradient",
    )(fall, kvf)
    return (att[None], dq[None], fg[None], weight_grad)


def solution(mesh):
    return jax.shard_map(
        local,
        mesh=mesh,
        in_specs=(P("dp", "seq", None), P("dp", "seq", None), P("dp", None), P("dp", "seq", None)),
        out_specs=(
            P("dp", "seq", None),
            P("dp", "seq", None),
            P("dp", "seq", None),
            P(("dp", "seq"), None),
        ),
        check_vma=False,
    )
```

time: 1390 us -> 199 us (0.14)
  waiting for transfers between devices: 1060 us -> 0 us
  Pallas kernels: 0 us -> 192 us
  matrix products: 126 us -> 0 us
  starting transfers between devices: 81.2 us -> 0 us
  local copies, waits for them, and re-layouts: 49.4 us -> 6.6 us
  blocking collectives: 25.9 us -> 0 us
  other arithmetic: 21 us -> 0 us
    unnamed x4 -> x0, waiting for transfers between devices: 655 us -> none
    ppermute x16 -> x0, waiting for transfers between devices: 214 us -> none  [passed_along(): lax.ppermute(value, axis, [(source, source + steps) for source in range(l...]
    pallas_call x0 -> x2, Pallas kernels: none -> 192 us  [the longest x1 136 us: local(): pl.pallas_call(attention_kernel, out_shape=(sds((256, 1024), BF), sds((25...]
    all_gather x2 -> x0, waiting for transfers between devices: 191 us -> none  [the longest x1 115 us: local(): full_weight = lax.all_gather(kv_weight, 'dp', axis=0, tiled=True)]
    dot_general x51 -> x0, matrix products: 126 us -> none  [the longest x8 20.1 us: head_work(): lax.dot_general(weights, grad_head, token_dims, preferred_element_type=jn...]
    ppermute x16 -> x0, starting transfers between devices: 81 us -> none  [passed_along(): lax.ppermute(value, axis, [(source, source + steps) for source in range(l...]
    unnamed x49 -> x14, local copies, waits for them, and re-layouts: 36.9 us -> 6.6 us
    all_to_all x1 -> x0, blocking collectives: 25.9 us -> none  [local(): lax.all_to_all(tokens, 'dp', split_axis=1, concat_axis=0, tiled=True)]
  transfers between devices with their start and end apart: 19 -> 0, of which waited for: 16 -> 0; matrix products, arithmetic and copies ran while one was open for 1% -> 0% of each run, Pallas kernels for 0% -> 0%
where the time goes in v1:
time: 199 us
  Pallas kernels  192 us (96%)
  local copies, waits for them, and re-layouts  6.6 us (3%)
    pallas_call x1, Pallas kernels, local(): pl.pallas_call(attention_kernel, out_shape=(sds((256, 1024), BF), sds((25...  136 us
    pallas_call x1, Pallas kernels, local(): pl.pallas_call(weight_kernel, out_shape=sds((8, 2048), F32), in_specs=[an...  56.1 us
    unnamed x14, local copies, waits for them, and re-layouts  6.6 us

profile of v1, /device:TPU:1, one launch (start us, length us, event | category | flops | bytes accessed | tf_op | source)
XLA Modules:
  0.0 199.1 jit_solution(7407964060654351234)
XLA Ops:
  0.6 135.8 %attention.1 = (bf16[256,1024]{1,0:T(8,128)(2,1)}, bf16[256,1024]{1,0:T(8,128)(2,1)}, bf16[256,2048]{1,0:T(8,128)(2,1)}, bf16[2,4,256,256]{3,2,1,0:T(8,128)(2,1)}, bf16[2,4,256,1024]{3,2,1,0:T(8,128)(2,1)}) custom-call(bf16[256,2048]{1,0:T(8,128)(2,1)} %bitcast.7, bf16[256,1024]{1,0:T(8,128)(2,1)} %bitcast.8, bf16[1024,2048]{1,0:T(8,128)(2,1)} %w_in.1, ...), custom_call_target="tpu_custom_call" | custom-call | tf_op jit(solution)/shard_map/attention/pallas_call | solution.py:555
  136.4 0.0 copy-start
  136.5 2.2 %copy-done = bf16[2,4,256,1024]{3,2,1,0:T(8,128)(2,1)S(1)} copy-done((bf16[2,4,256,1024]{3,2,1,0:T(8,128)(2,1)S(1)}, bf16[2,4,256,1024]{3,2,1,0:T(8,128)(2,1)}, u32[]{:S(2)}) %copy-start) | copy-done | bytes 4194328
  138.6 0.0 copy-start.1
  138.6 1.2 copy-done.1
  139.9 0.0 copy-start.4
  139.9 0.0 copy-start.3
  139.9 0.0 copy-start.2
  139.9 56.1 %weight_gradient.1 = f32[8,2048]{1,0:T(8,128)S(1)} custom-call(bf16[2,4,256,1024]{3,2,1,0:T(8,128)(2,1)S(1)} %copy-done, bf16[2,4,256,256]{3,2,1,0:T(8,128)(2,1)S(1)} %copy-done.1), custom_call_target="tpu_custom_call" | custom-call | tf_op jit(solution)/shard_map/weight_gradient/pallas_call | solution.py:593
  195.9 0.0 copy-done.4
  195.9 0.8 copy.12
  196.7 0.0 copy-done.3
  196.7 0.8 copy.13
  197.5 0.0 copy-done.2
  197.5 1.0 copy.14
  198.5 0.6 copy.15
Async XLA Ops:
  136.4 2.2 %copy-start = (bf16[2,4,256,1024]{3,2,1,0:T(8,128)(2,1)S(1)}, bf16[2,4,256,1024]{3,2,1,0:T(8,128)(2,1)}, u32[]{:S(2)}) copy-start(bf16[2,4,256,1024]{3,2,1,0:T(8,128)(2,1)} %get-tuple-element.12.fall_in) | copy-start | bytes 12582916
  138.6 1.2 copy-start.1
  139.9 56.1 %copy-start.4 = (bf16[256,1024]{1,0:T(8,128)(2,1)S(1)}, bf16[256,1024]{1,0:T(8,128)(2,1)}, u32[]{:S(2)}) copy-start(bf16[256,1024]{1,0:T(8,128)(2,1)} %get-tuple-element.9) | copy-start | bytes 1572868
  139.9 56.9 %copy-start.3 = (bf16[256,1024]{1,0:T(8,128)(2,1)S(1)}, bf16[256,1024]{1,0:T(8,128)(2,1)}, u32[]{:S(2)}) copy-start(bf16[256,1024]{1,0:T(8,128)(2,1)} %get-tuple-element.10) | copy-start | bytes 1572868
  139.9 57.7 %copy-start.2 = (bf16[256,2048]{1,0:T(8,128)(2,1)S(1)}, bf16[256,2048]{1,0:T(8,128)(2,1)}, u32[]{:S(2)}) copy-start(bf16[256,2048]{1,0:T(8,128)(2,1)} %get-tuple-element.11) | copy-start | bytes 3145732

commit v2 on v1

--- a/solution.py
+++ b/solution.py
@@ -17,7 +17,6 @@
 SCALE = 1.0 / math.sqrt(HD)
 EXP_SCALE = SCALE * math.log2(math.e)
 NT = (((1,), (1,)), ((), ()))
-TN = (((0,), (0,)), ((), ()))
 
 
 def loop(lo, hi, body):
@@ -50,13 +49,18 @@
 
 def attention_kernel(
     x_in, q_in, w_in, up_in,
-    att_out, dq_out, fg_out, kvf_out, fall_out,
-    wf, xv, stage, kbuf, kvt, qbuf, s_ref, dp_ref, dkv, sbuf, rbuf, kvf, kvg, obuf, fgv,
+    att_out, dq_out, fg_out, dw_out,
+    wf, xv, xt, stage, kbuf, kvt, qbuf, s_ref, dp_ref, dkv, sbuf, rbuf, kvf, kvp, kvg, obuf, fgv,
+    fv, dwa, dwb, r1, dz, r2, s3, r3,
     wl, ws, wr, wfs, wfr, xl, ks, kr, kl, hs, hr, qs, qr, ql, fs, fr, fl,
     os_, or_, ol, rs, rr, gs, gr, gl, el,
+    ps, pr, s1s, s1r, s2s, s2r, s3s, s3r,
 ):
     n_seq = lax.axis_size("seq")
+    n_z = n_seq // 16
     seq, dp, me, base = place()
+    xi = (seq // 4) % 4
+    zi = seq // 16
     core = seq % 2
     y_hi = (seq // 2) % 2
     other = 1 - dp
@@ -137,17 +141,17 @@
         src, dst = q_copy(hl, me, which)
         return pltpu.make_async_copy(src, dst, ql.at[hl, which])
 
-    def x_cols(which_dp):
-        return x_in.at[:, pl.ds(pl.multiple_of(which_dp * 1024, 1024), 1024)]
+    def x_part(which_dp):
+        return xt.at[pl.ds(pl.multiple_of(which_dp * 1024, 1024), 1024), :]
 
     def f_send(j, d):
-        return remote(x_cols(d), fall_out.at[dp, me], fs.at[d, j], fr.at[dp, me], base + j, d)
+        return remote(x_part(d), fv.at[dp, me], fs.at[d, j], fr.at[dp, me], base + j, d)
 
     def f_arrive(j, d):
-        return remote(x_cols(d), fall_out.at[d, j], fs.at[d, j], fr.at[d, j], base + j, d)
+        return remote(x_part(d), fv.at[d, j], fs.at[d, j], fr.at[d, j], base + j, d)
 
     def f_local():
-        return pltpu.make_async_copy(x_cols(dp), fall_out.at[dp, me], fl)
+        return pltpu.make_async_copy(x_part(dp), fv.at[dp, me], fl)
 
     def o_send(hl, j, which):
         out = (att_out, dq_out)[which]
@@ -188,6 +192,37 @@
 
     def g_local(hl):
         return pltpu.make_async_copy(kvf.at[hl, me], kvg.at[hl * 4 + me], gl.at[hl])
+
+    def p_send(hl, i):
+        return remote(kvf.at[hl, i], kvp.at[hl, i], ps.at[hl, i], pr.at[hl, i], seq, other)
+
+    def x_seq(x):
+        return zi * 16 + x * 4 + me
+
+    def z_seq(z):
+        return z * 16 + xi * 4 + me
+
+    def first(hl, x):
+        return remote(
+            dwb.at[hl, x], r1.at[hl, xi], s1s.at[hl, x], s1r.at[hl, xi], x_seq(x), dp
+        )
+
+    def first_arrive(hl, x):
+        return remote(dwb.at[hl, x], r1.at[hl, x], s1s.at[hl, x], s1r.at[hl, x], x_seq(x), dp)
+
+    def second(hl, z):
+        return remote(
+            dz.at[hl, z], r2.at[hl, zi], s2s.at[hl, z], s2r.at[hl, zi], z_seq(z), dp
+        )
+
+    def second_arrive(hl, z):
+        return remote(dz.at[hl, z], r2.at[hl, z], s2s.at[hl, z], s2r.at[hl, z], z_seq(z), dp)
+
+    def third(j):
+        return remote(s3.at[j], r3.at[me], s3s.at[j], s3r.at[me], base + j, dp)
+
+    def third_arrive(j):
+        return remote(s3.at[j], r3.at[j], s3s.at[j], s3r.at[j], base + j, dp)
 
     def others(body):
         loop(1, 4, lambda r: body((me + r) % 4))
@@ -234,11 +269,6 @@
         others(one)
 
     def attend(hl):
-        def clear(b):
-            dkv[hl, b] = jnp.zeros((BLK, 2 * HD), F32)
-            kvt[b] = kbuf[hl, b].T
-
-        loop(0, 12, clear)
         rows = lax.broadcasted_iota(jnp.int32, (BLK, BLK), 0)
         columns = lax.broadcasted_iota(jnp.int32, (BLK, BLK), 1)
 
@@ -283,8 +313,8 @@
                 dscore = ((e * inverse_scaled) * (dp_ref[w] - mean)).astype(BF)
                 dkv[hl, qi + w, :, :HD] += jnp.dot(dscore, query, preferred_element_type=F32)
                 dkv[hl, qi + w, :, HD:] += jnp.dot(weights, grad, preferred_element_type=F32)
-                att = att + jnp.dot(kvt[qi + w, HD:, :], weights, preferred_element_type=F32)
-                dq = dq + jnp.dot(kvt[qi + w, :HD, :], dscore, preferred_element_type=F32)
+                att = att + jnp.dot(kvt[hl, qi + w, HD:, :], weights, preferred_element_type=F32)
+                dq = dq + jnp.dot(kvt[hl, qi + w, :HD, :], dscore, preferred_element_type=F32)
             obuf[hl, qi, :, :HD] = att.T.astype(BF)
             obuf[hl, qi, :, HD:] = dq.T.astype(BF)
 
@@ -315,6 +345,7 @@
             back(hl, i, 1).wait_recv()
             whole = dkv[hl, SPAN + i] + rbuf[hl, 0, i].astype(F32) + rbuf[hl, 1, i].astype(F32)
             kvf[hl, i] = whole.astype(BF)
+            p_send(hl, i).start()
 
             @pl.when(i == me)
             def _():
@@ -326,16 +357,57 @@
 
         loop(0, 4, one)
 
-    x_copy = pltpu.make_async_copy(x_in, xv, xl)
-    x_copy.start()
-    for hl in range(2):
-        for kv in range(2):
-            loop(0, 4, lambda j: w_local(hl, j, kv).start())
-    greet(
-        [(base + (me + r) % 4, dp) for r in range(4) if r]
-        + [(base + (me + r) % 4, other) for r in range(4)]
-        + [(near_next, dp), (far_next, dp), (near_prev, dp), (far_prev, dp)]
-    )
+    def product(hl, t, sample, kv):
+        at = pl.multiple_of(t * 256, 256)
+        acc = jnp.zeros((256, 2 * HD), F32)
+        for b in range(4):
+            acc = acc + jnp.dot(
+                fv[sample, b, pl.ds(at, 256), :], kv[hl, b], preferred_element_type=F32
+            )
+        return acc
+
+    def product_own(hl):
+        def tile(t):
+            dwa[t] = product(hl, t, dp, kvf)
+
+        loop(0, 4, tile)
+
+    def product_other(hl):
+        loop(0, 4, lambda i: p_send(hl, i).wait_recv())
+
+        def tile(t):
+            acc = dwa[t] + product(hl, t, other, kvp)
+            for zz in range(2):
+                for xx in range(4):
+                    lo = (zz * 4 + xx) * 32
+                    dwb[hl, xx, 2 * t + zz] = acc[lo:lo + 32].astype(BF)
+
+        loop(0, 4, tile)
+        loop(1, 4, lambda r: first(hl, (xi + r) % 4).start())
+
+    def add_x(hl, z):
+        acc = dwb[hl, xi, z].astype(F32)
+        for r in range(1, 4):
+            acc = acc + r1[hl, (xi + r) % 4, z].astype(F32)
+        return acc
+
+    def second_stage(hl):
+        loop(1, 4, lambda r: first_arrive(hl, (xi + r) % 4).wait_recv())
+
+        def one(r):
+            z = (zi + r) % n_z
+            dz[hl, z] = add_x(hl, z).astype(BF)
+            second(hl, z).start()
+
+        loop(1, n_z, one)
+
+    def third_stage(hl):
+        acc = add_x(hl, zi)
+        loop(1, n_z, lambda r: second_arrive(hl, (zi + r) % n_z).wait_recv())
+        for r in range(1, n_z):
+            acc = acc + r2[hl, (zi + r) % n_z].astype(F32)
+        for j in range(4):
+            s3[j, :, hl * 256:(hl + 1) * 256] = acc[j * 8:(j + 1) * 8]
 
     def w_start(hl):
         def one(j):
@@ -354,25 +426,23 @@
 
         others(one)
 
-    w_start(0)
-    x_copy.wait()
-    project(0)
-    others(lambda j: kv_send(0, j).wait_send())
-    w_start(1)
-    q_start(0)
-    send_halo(0)
-    project(1)
-    q_start(1)
-    send_halo(1)
-    f_local().start()
-    loop(1, 8, lambda t: f_send((me + t % 4) % 4, (dp + t // 4) % 2).start())
+    def turn(hl, b):
+        dkv[hl, b] = jnp.zeros((BLK, 2 * HD), F32)
+        kvt[hl, b] = kbuf[hl, b].T
 
     def ready(hl):
-        def one(i):
+        loop(SPAN, SPAN + 4, lambda b: turn(hl, b))
+
+        def near(i):
             halo(hl, i, 0).wait_recv()
+            turn(hl, 4 + i)
+
+        def far(i):
             halo(hl, i, 1).wait_recv()
-
-        loop(0, 4, one)
+            turn(hl, i)
+
+        loop(0, 4, near)
+        loop(0, 4, far)
         q_local(hl, 0).wait()
         q_local(hl, 1).wait()
 
@@ -381,18 +451,6 @@
             q_arrive(hl, j, 1).wait_recv()
 
         others(two)
-
-    ready(0)
-    attend(0)
-    ready(1)
-    attend(1)
-    finish(0)
-    finish(1)
-    kvf_copy = pltpu.make_async_copy(kvf, kvf_out, el.at[0])
-    kvf_copy.start()
-    for hl in range(2):
-        g_local(hl).wait()
-        others(lambda j: g_arrive(hl, j).wait_recv())
 
     def feature(n):
         at = pl.multiple_of(n * 256, 256)
@@ -403,134 +461,58 @@
             )
         fgv[:, pl.ds(at, 256)] = acc.astype(BF)
 
-    loop(0, 8, feature)
-    fg_copy = pltpu.make_async_copy(fgv, fg_out, el.at[1])
-    fg_copy.start()
-
+    x_copy = pltpu.make_async_copy(x_in, xv, xl)
+    x_copy.start()
     for hl in range(2):
-        def w_end(j):
-            w_send(hl, j, 0).wait_send()
-            w_send(hl, j, 1).wait_send()
-            w_swap(hl, j, core).wait_send()
-
-        loop(0, 4, w_end)
-
-        def four_end(i):
-            for far in range(2):
-                halo(hl, i, far).wait_send()
-                back(hl, i, far).wait_send()
-
-        loop(0, 4, four_end)
-
-        def three_end(j):
-            if hl == 1:
-                kv_send(hl, j).wait_send()
-            g_send(hl, j).wait_send()
-            for which in range(2):
-                q_send(hl, j, which).wait_send()
-                o_send(hl, j, which).wait_send()
-                o_arrive(hl, j, which).wait_recv()
-
-        others(three_end)
-        o_local(hl, 0).wait()
-        o_local(hl, 1).wait()
-    f_local().wait()
-
-    def f_end(t):
-        j, d = (me + t % 4) % 4, (dp + t // 4) % 2
-        f_send(j, d).wait_send()
-        f_arrive(j, d).wait_recv()
-
-    loop(1, 8, f_end)
-    kvf_copy.wait()
-    fg_copy.wait()
-
-
-def weight_kernel(
-    fall_in, kvf_in, dw_out,
-    fv, gv, dwb, r1, dz, r2, s3, r3,
-    il, ps, pr, s1s, s1r, s2s, s2r, s3s, s3r,
-):
-    n_z = lax.axis_size("seq") // 16
-    seq, dp, me, base = place()
-    xi = (seq // 4) % 4
-    zi = seq // 16
-    other = 1 - dp
-
-    f_copy = pltpu.make_async_copy(fall_in, fv, il.at[0])
-    g_copy = pltpu.make_async_copy(kvf_in, gv.at[dp], il.at[1])
-    f_copy.start()
-    g_copy.start()
-    x_seq = lambda x: zi * 16 + x * 4 + me
-    z_seq = lambda z: z * 16 + xi * 4 + me
+        for kv in range(2):
+            loop(0, 4, lambda j: w_local(hl, j, kv).start())
     greet(
-        [(seq, other)]
-        + [(base + (me + r) % 4, dp) for r in range(1, 4)]
+        [(base + (me + r) % 4, dp) for r in range(1, 4)]
+        + [(base + (me + r) % 4, other) for r in range(4)]
+        + [(near_next, dp), (far_next, dp), (near_prev, dp), (far_prev, dp)]
         + [(x_seq((xi + r) % 4), dp) for r in range(1, 4)]
         + [(z_seq((zi + r) % n_z), dp) for r in range(1, n_z)]
     )
-    p_copy = remote(kvf_in, gv.at[dp], ps, pr, seq, other)
-    p_copy.start()
-    f_copy.wait()
-    g_copy.wait()
-    remote(kvf_in, gv.at[other], ps, pr, seq, other).wait_recv()
-
-    def tile(t):
+    w_start(0)
+    x_copy.wait()
+
+    def flip(t):
         at = pl.multiple_of(t * 256, 256)
-        for hl in range(2):
-            acc = jnp.zeros((256, 2 * HD), F32)
-            for s in range(2):
-                for b in range(4):
-                    acc = acc + lax.dot_general(
-                        fv[s, b, :, pl.ds(at, 256)], gv[s, hl, b], TN, preferred_element_type=F32
-                    )
-            for zz in range(2):
-                for xx in range(4):
-                    lo = (zz * 4 + xx) * 32
-                    dwb[xx, 2 * t + zz, :, hl * 256:(hl + 1) * 256] = acc[lo:lo + 32].astype(BF)
-
-    loop(0, 4, tile)
-
-    def first(x):
-        return remote(dwb.at[x], r1.at[xi], s1s.at[x], s1r.at[xi], x_seq(x), dp)
-
-    def first_arrive(x):
-        return remote(dwb.at[x], r1.at[x], s1s.at[x], s1r.at[x], x_seq(x), dp)
-
-    loop(1, 4, lambda r: first((xi + r) % 4).start())
-    loop(1, 4, lambda r: first_arrive((xi + r) % 4).wait_recv())
-
-    def second(z):
-        return remote(dz.at[z], r2.at[zi], s2s.at[z], s2r.at[zi], z_seq(z), dp)
-
-    def second_arrive(z):
-        return remote(dz.at[z], r2.at[z], s2s.at[z], s2r.at[z], z_seq(z), dp)
-
-    def add_x(z):
-        acc = dwb[xi, z].astype(F32)
-        for r in range(1, 4):
-            acc = acc + r1[(xi + r) % 4, z].astype(F32)
-        return acc
-
-    def one_z(r):
-        z = (zi + r) % n_z
-        dz[z] = add_x(z).astype(BF)
-        second(z).start()
-
-    loop(1, n_z, one_z)
-    acc = add_x(zi)
-    loop(1, n_z, lambda r: second_arrive((zi + r) % n_z).wait_recv())
-    for r in range(1, n_z):
-        acc = acc + r2[(zi + r) % n_z].astype(F32)
-    for j in range(4):
-        s3[j] = acc[j * 8:(j + 1) * 8]
-
-    def third(j):
-        return remote(s3.at[j], r3.at[me], s3s.at[j], s3r.at[me], base + j, dp)
-
-    def third_arrive(j):
-        return remote(s3.at[j], r3.at[j], s3s.at[j], s3r.at[j], base + j, dp)
-
+        xt[pl.ds(at, 256), :] = xv[:, pl.ds(at, 256)].T
+
+    loop(0, 8, flip)
+    project(0)
+    others(lambda j: kv_send(0, j).wait_send())
+    w_start(1)
+    send_halo(0)
+    project(1)
+    q_start(0)
+    q_start(1)
+    send_halo(1)
+    f_local().start()
+    loop(1, 8, lambda t: f_send((me + t % 4) % 4, (dp + t // 4) % 2).start())
+    ready(0)
+    attend(0)
+    ready(1)
+    attend(1)
+    finish(0)
+    f_local().wait()
+    loop(1, 8, lambda t: f_arrive((me + t % 4) % 4, (dp + t // 4) % 2).wait_recv())
+    product_own(0)
+    finish(1)
+    product_other(0)
+    product_own(1)
+    for hl in range(2):
+        g_local(hl).wait()
+        others(lambda j: g_arrive(hl, j).wait_recv())
+    product_other(1)
+    second_stage(0)
+    loop(0, 8, feature)
+    fg_copy = pltpu.make_async_copy(fgv, fg_out, el)
+    fg_copy.start()
+    second_stage(1)
+    third_stage(0)
+    third_stage(1)
     loop(1, 4, lambda r: third((me + r) % 4).start())
     r3[me] = s3[me]
     loop(1, 4, lambda r: third_arrive((me + r) % 4).wait_recv())
@@ -541,31 +523,59 @@
                 lo = hl * 256 + kv * HD
                 dw_out[:, head:head + HD] = r3[j, :, lo:lo + HD]
 
-    p_copy.wait_send()
-    loop(1, 4, lambda r: first((xi + r) % 4).wait_send())
-    loop(1, n_z, lambda r: second((zi + r) % n_z).wait_send())
+    for hl in range(2):
+        def w_end(j):
+            w_send(hl, j, 0).wait_send()
+            w_send(hl, j, 1).wait_send()
+            w_swap(hl, j, core).wait_send()
+
+        loop(0, 4, w_end)
+
+        def four_end(i):
+            for far in range(2):
+                halo(hl, i, far).wait_send()
+                back(hl, i, far).wait_send()
+            p_send(hl, i).wait_send()
+
+        loop(0, 4, four_end)
+
+        def three_end(j):
+            if hl == 1:
+                kv_send(hl, j).wait_send()
+            g_send(hl, j).wait_send()
+            for which in range(2):
+                q_send(hl, j, which).wait_send()
+                o_send(hl, j, which).wait_send()
+                o_arrive(hl, j, which).wait_recv()
+
+        others(three_end)
+        o_local(hl, 0).wait()
+        o_local(hl, 1).wait()
+        loop(1, 4, lambda r: first(hl, (xi + r) % 4).wait_send())
+        loop(1, n_z, lambda r: second(hl, (zi + r) % n_z).wait_send())
+    loop(1, 8, lambda t: f_send((me + t % 4) % 4, (dp + t // 4) % 2).wait_send())
     loop(1, 4, lambda r: third((me + r) % 4).wait_send())
+    fg_copy.wait()
 
 
 def local(features, queries, kv_weight, upstream):
     dma = pltpu.SemaphoreType.DMA
     anywhere = pl.BlockSpec(memory_space=pl.ANY)
-    vmem = pl.BlockSpec(memory_space=pltpu.VMEM)
     sds = jax.ShapeDtypeStruct
-    att, dq, fg, kvf, fall = pl.pallas_call(
+    att, dq, fg, dw = pl.pallas_call(
         attention_kernel,
         out_shape=(
-            sds((256, 1024), BF), sds((256, 1024), BF), sds((256, 2048), BF),
-            sds((2, 4, 256, 256), BF), sds((2, 4, 256, 1024), BF),
+            sds((256, 1024), BF), sds((256, 1024), BF), sds((256, 2048), BF), sds((8, 2048), F32),
         ),
         in_specs=[anywhere] * 4,
-        out_specs=(anywhere,) * 5,
+        out_specs=(anywhere, anywhere, anywhere, pl.BlockSpec(memory_space=pltpu.VMEM)),
         scratch_shapes=[
             pltpu.VMEM((8, 2048, 256), BF),
             pltpu.VMEM((256, 2048), BF),
+            pltpu.VMEM((2048, 256), BF),
             pltpu.VMEM((8, 256, 256), BF),
             pltpu.VMEM((2, 12, 256, 256), BF),
-            pltpu.VMEM((12, 256, 256), BF),
+            pltpu.VMEM((2, 12, 256, 256), BF),
             pltpu.VMEM((2, 4, 256, 256), BF),
             pltpu.VMEM((9, 256, 256), F32),
             pltpu.VMEM((9, 256, 256), F32),
@@ -573,9 +583,18 @@
             pltpu.VMEM((2, 8, 256, 256), BF),
             pltpu.VMEM((2, 2, 4, 256, 256), BF),
             pltpu.VMEM((2, 4, 256, 256), BF),
+            pltpu.VMEM((2, 4, 256, 256), BF),
             pltpu.VMEM((8, 256, 256), BF),
             pltpu.VMEM((2, 4, 256, 256), BF),
             pltpu.VMEM((256, 2048), BF),
+            pltpu.VMEM((2, 4, 1024, 256), BF),
+            pltpu.VMEM((4, 256, 256), F32),
+            pltpu.VMEM((2, 4, 8, 32, 256), BF),
+            pltpu.VMEM((2, 4, 8, 32, 256), BF),
+            pltpu.VMEM((2, 8, 32, 256), BF),
+            pltpu.VMEM((2, 8, 32, 256), BF),
+            pltpu.VMEM((4, 8, 512), F32),
+            pltpu.VMEM((4, 8, 512), F32),
             dma((8, 2)), dma((8, 2)), dma((8, 2)), dma((8,)), dma((8,)), dma,
             dma((2, 4)), dma((2, 4)), dma((2,)),
             dma((2, 2, 4)), dma((2, 2, 4)),
@@ -583,36 +602,16 @@
             dma((2, 4)), dma((2, 4)), dma,
             dma((2, 4, 2)), dma((2, 4, 2)), dma((2, 2)),
             dma((2, 2, 4)), dma((2, 2, 4)),
-            dma((2, 4)), dma((2, 4)), dma((2,)), dma((2,)),
+            dma((2, 4)), dma((2, 4)), dma((2,)), dma,
+            dma((2, 4)), dma((2, 4)),
+            dma((2, 4)), dma((2, 4)), dma((2, 8)), dma((2, 8)), dma((4,)), dma((4,)),
         ],
         compiler_params=pltpu.CompilerParams(
-            collective_id=0, has_side_effects=True, vmem_limit_bytes=56 << 20
+            collective_id=0, has_side_effects=True, vmem_limit_bytes=58 << 20
         ),
         name="attention",
     )(features[0], queries[0], kv_weight, upstream[0])
-    weight_grad = pl.pallas_call(
-        weight_kernel,
-        out_shape=sds((8, 2048), F32),
-        in_specs=[anywhere] * 2,
-        out_specs=vmem,
-        scratch_shapes=[
-            pltpu.VMEM((2, 4, 256, 1024), BF),
-            pltpu.VMEM((2, 2, 4, 256, 256), BF),
-            pltpu.VMEM((4, 8, 32, 512), BF),
-            pltpu.VMEM((4, 8, 32, 512), BF),
-            pltpu.VMEM((8, 32, 512), BF),
-            pltpu.VMEM((8, 32, 512), BF),
-            pltpu.VMEM((4, 8, 512), F32),
-            pltpu.VMEM((4, 8, 512), F32),
-            dma((2,)), dma, dma,
-            dma((4,)), dma((4,)), dma((8,)), dma((8,)), dma((4,)), dma((4,)),
-        ],
-        compiler_params=pltpu.CompilerParams(
-            collective_id=1, has_side_effects=True, vmem_limit_bytes=40 << 20
-        ),
-        name="weight_gradient",
-    )(fall, kvf)
-    return (att[None], dq[None], fg[None], weight_grad)
+    return (att[None], dq[None], fg[None], dw)
 
 
 def solution(mesh):

time: 199 us -> 184 us (0.925)
  Pallas kernels: 192 us -> 177 us
    pallas_call x1 -> x0, Pallas kernels: 56.1 us -> none  [local(): pl.pallas_call(weight_kernel, out_shape=sds((8, 2048), F32), in_specs=[an...]
    pallas_call x1, Pallas kernels: 136 us -> 177 us  [local(): pl.pallas_call(attention_kernel, out_shape=(sds((256, 1024), BF), sds((25...]
    unnamed x14 -> x6, local copies, waits for them, and re-layouts: 6.6 us -> 6.7 us
where the time goes in v2:
time: 184 us
  Pallas kernels  177 us (96%)
  local copies, waits for them, and re-layouts  6.7 us (4%)
    pallas_call x1, Pallas kernels, local(): pl.pallas_call(attention_kernel, out_shape=(sds((256, 1024), BF), sds((25...  177 us
    unnamed x6, local copies, waits for them, and re-layouts  6.7 us

profile of v2, /device:TPU:1, one launch (start us, length us, event | category | flops | bytes accessed | tf_op | source)
XLA Modules:
  0.0 184.0 jit_solution(9784247599962056486)
XLA Ops:
  0.6 176.7 %attention.1 = (bf16[256,1024]{1,0:T(8,128)(2,1)}, bf16[256,1024]{1,0:T(8,128)(2,1)}, bf16[256,2048]{1,0:T(8,128)(2,1)}, f32[8,2048]{1,0:T(8,128)}) custom-call(bf16[256,2048]{1,0:T(8,128)(2,1)} %bitcast.7, bf16[256,1024]{1,0:T(8,128)(2,1)} %bitcast.8, bf16[1024,2048]{1,0:T(8,128)(2,1)} %w_in.1, bf16[256,1024]{1,0:T(8,128)(2,1)} %bitcast.9), custom_call_target="tpu_custom_call" | custom-call | tf_op jit(solution)/shard_map/attention/pallas_call | solution.py:565
  177.3 0.0 copy-start
  177.3 1.9 %copy.12 = bf16[1,256,1024]{2,1,0:T(8,128)(2,1)} copy(bf16[1,256,1024]{2,1,0:T(8,128)(2,1)} %bitcast.11) | data formatting | bytes 1048576
  179.2 1.9 %copy.13 = bf16[1,256,1024]{2,1,0:T(8,128)(2,1)} copy(bf16[1,256,1024]{2,1,0:T(8,128)(2,1)} %bitcast.10) | data formatting | bytes 1048576
  181.1 2.3 %copy.14 = bf16[1,256,2048]{2,1,0:T(8,128)(2,1)} copy(bf16[1,256,2048]{2,1,0:T(8,128)(2,1)} %bitcast.6) | data formatting | bytes 2097152
  183.4 0.0 copy-done
  183.4 0.6 copy.15
Async XLA Ops:
  177.3 6.1 %copy-start = (f32[8,2048]{1,0:T(8,128)S(1)}, f32[8,2048]{1,0:T(8,128)}, u32[]{:S(2)}) copy-start(f32[8,2048]{1,0:T(8,128)} %get-tuple-element.19) | copy-start | bytes 196612

commit v3 on v2

--- a/solution.py
+++ b/solution.py
@@ -44,7 +44,7 @@
     barrier = pltpu.get_barrier_semaphore()
     for seq, dp in partners:
         pl.semaphore_signal(barrier, inc=1, device_id={"seq": seq, "dp": dp}, device_id_type=MESH)
-    pl.semaphore_wait(barrier, len(partners))
+    return lambda: pl.semaphore_wait(barrier, len(partners))
 
 
 def attention_kernel(
@@ -52,7 +52,7 @@
     att_out, dq_out, fg_out, dw_out,
     wf, xv, xt, stage, kbuf, kvt, qbuf, s_ref, dp_ref, dkv, sbuf, rbuf, kvf, kvp, kvg, obuf, fgv,
     fv, dwa, dwb, r1, dz, r2, s3, r3,
-    wl, ws, wr, wfs, wfr, xl, ks, kr, kl, hs, hr, qs, qr, ql, fs, fr, fl,
+    wl, ws, wr, wfs, wfr, xl, ks, kr, kl, hs, hr, qs, qr, ql, fs, fr, fl, fps, fpr,
     os_, or_, ol, rs, rr, gs, gr, gl, el,
     ps, pr, s1s, s1r, s2s, s2r, s3s, s3r,
 ):
@@ -64,10 +64,12 @@
     core = seq % 2
     y_hi = (seq // 2) % 2
     other = 1 - dp
-    up_y = (y_hi + dp) % 2
-    down_y = (y_hi + 1 - dp) % 2
-    up_seq = base + up_y * 2 + core
-    down_seq = base + down_y * 2 + core
+
+    def owner(position, which_dp):
+        return (position + 2 * which_dp * (position % 2)) % 4
+
+    mine = owner(me, dp)
+    twin_seq = base + owner(mine, other)
     w_seq = base + ((y_hi + (1 - dp) * (1 - core) + dp * core) % 2) * 2 + core
     pair_seq = base + y_hi * 2 + (1 - core)
     near_next = (seq + 4) % n_seq
@@ -99,27 +101,31 @@
         part = wf.at[hl * 4 + j, w_rows(other, core), pl.ds(kv * HD, HD)]
         return remote(part, part, ws.at[hl * 4 + j, kv], wr.at[hl * 4 + j, kv], w_seq, other)
 
-    def w_swap(hl, j, which_core):
-        part = wf.at[hl * 4 + j, w_rows(other, which_core), :]
-        return remote(part, part, wfs.at[hl * 4 + j], wfr.at[hl * 4 + j], pair_seq, dp)
-
-    def kv_send(hl, j):
-        return remote(
-            stage.at[hl * 4 + j], kbuf.at[hl, SPAN + me], ks.at[hl, j], kr.at[hl, me], base + j, dp
-        )
-
-    def kv_arrive(hl, j):
-        return remote(
-            stage.at[hl * 4 + j], kbuf.at[hl, SPAN + j], ks.at[hl, j], kr.at[hl, j], base + j, dp
-        )
-
-    def kv_local(hl):
-        return pltpu.make_async_copy(stage.at[hl * 4 + me], kbuf.at[hl, SPAN + me], kl.at[hl])
-
-    def halo(hl, i, far):
-        return remote(
-            kbuf.at[hl, SPAN + i], kbuf.at[hl, (1 - far) * 4 + i],
-            hs.at[hl, far, i], hr.at[hl, far, i], far_next if far else near_next, dp,
+    def w_swap(hl, j, kv, which_core):
+        part = wf.at[hl * 4 + j, w_rows(other, which_core), pl.ds(kv * HD, HD)]
+        return remote(part, part, wfs.at[hl * 4 + j, kv], wfr.at[hl * 4 + j, kv], pair_seq, dp)
+
+    def kv_send(hl, kv, j):
+        return remote(
+            stage.at[kv, hl * 4 + j], kbuf.at[hl, kv, SPAN + me],
+            ks.at[hl, kv, j], kr.at[hl, kv, me], base + owner(j, dp), dp,
+        )
+
+    def kv_arrive(hl, kv, i):
+        return remote(
+            stage.at[kv, hl * 4 + i], kbuf.at[hl, kv, SPAN + i],
+            ks.at[hl, kv, i], kr.at[hl, kv, i], base + i, dp,
+        )
+
+    def kv_local(hl, kv):
+        return pltpu.make_async_copy(
+            stage.at[kv, hl * 4 + mine], kbuf.at[hl, kv, SPAN + me], kl.at[hl, kv]
+        )
+
+    def halo(hl, kv, i, far):
+        return remote(
+            kbuf.at[hl, kv, SPAN + i], kbuf.at[hl, kv, (1 - far) * 4 + i],
+            hs.at[hl, kv, far, i], hr.at[hl, kv, far, i], far_next if far else near_next, dp,
         )
 
     def q_copy(hl, j, which):
@@ -128,49 +134,65 @@
 
     def q_send(hl, j, which):
         src, dst = q_copy(hl, j, which)
-        return remote(src, dst, qs.at[hl, j, which], qr.at[hl, me, which], base + j, dp)
-
-    def q_arrive(hl, j, which):
-        src, _ = q_copy(hl, j, which)
-        return remote(
-            src, qbuf.at[hl, j, :, pl.ds(which * HD, HD)],
-            qs.at[hl, j, which], qr.at[hl, j, which], base + j, dp,
+        return remote(
+            src, dst, qs.at[hl, j, which], qr.at[hl, me, which], base + owner(j, dp), dp
+        )
+
+    def q_arrive(hl, i, which):
+        src, _ = q_copy(hl, mine, which)
+        return remote(
+            src, qbuf.at[hl, i, :, pl.ds(which * HD, HD)],
+            qs.at[hl, i, which], qr.at[hl, i, which], base + i, dp,
         )
 
     def q_local(hl, which):
-        src, dst = q_copy(hl, me, which)
+        src, dst = q_copy(hl, mine, which)
         return pltpu.make_async_copy(src, dst, ql.at[hl, which])
 
     def x_part(which_dp):
         return xt.at[pl.ds(pl.multiple_of(which_dp * 1024, 1024), 1024), :]
 
-    def f_send(j, d):
-        return remote(x_part(d), fv.at[dp, me], fs.at[d, j], fr.at[dp, me], base + j, d)
-
-    def f_arrive(j, d):
-        return remote(x_part(d), fv.at[d, j], fs.at[d, j], fr.at[d, j], base + j, d)
+    def chip(t):
+        return (y_hi + t % 2) % 2, (dp + t // 2) % 2
+
+    def f_send(t):
+        y, d = chip(t)
+        return remote(
+            x_part(d), fv.at[dp, me], fs.at[d, y], fr.at[dp, y_hi], base + y * 2 + core, d
+        )
+
+    def f_arrive(t):
+        y, d = chip(t)
+        return remote(
+            x_part(d), fv.at[d, y * 2 + core], fs.at[d, y], fr.at[d, y], base + y * 2 + core, d
+        )
 
     def f_local():
         return pltpu.make_async_copy(x_part(dp), fv.at[dp, me], fl)
 
-    def o_send(hl, j, which):
+    def f_pass(t, which_core):
+        y, d = chip(t)
+        part = fv.at[d, y * 2 + which_core]
+        return remote(part, part, fps.at[d, y], fpr.at[d, y], pair_seq, dp)
+
+    def o_send(hl, i, which):
         out = (att_out, dq_out)[which]
         return remote(
-            obuf.at[hl, j, :, pl.ds(which * HD, HD)], out.at[:, cols(2 * me + hl, 0)],
-            os_.at[hl, j, which], or_.at[hl, me, which], base + j, dp,
+            obuf.at[hl, i, :, pl.ds(which * HD, HD)], out.at[:, cols(2 * mine + hl, 0)],
+            os_.at[hl, i, which], or_.at[hl, mine, which], base + i, dp,
         )
 
     def o_arrive(hl, j, which):
         out = (att_out, dq_out)[which]
         return remote(
             obuf.at[hl, j, :, pl.ds(which * HD, HD)], out.at[:, cols(2 * j + hl, 0)],
-            os_.at[hl, j, which], or_.at[hl, j, which], base + j, dp,
+            os_.at[hl, j, which], or_.at[hl, j, which], base + owner(j, dp), dp,
         )
 
     def o_local(hl, which):
         out = (att_out, dq_out)[which]
         return pltpu.make_async_copy(
-            obuf.at[hl, me, :, pl.ds(which * HD, HD)], out.at[:, cols(2 * me + hl, 0)],
+            obuf.at[hl, me, :, pl.ds(which * HD, HD)], out.at[:, cols(2 * mine + hl, 0)],
             ol.at[hl, which],
         )
 
@@ -180,21 +202,23 @@
             rs.at[hl, far, i], rr.at[hl, far, i], far_prev if far else near_prev, dp,
         )
 
-    def g_send(hl, j):
-        return remote(
-            kvf.at[hl, j], kvg.at[hl * 4 + me], gs.at[hl, j], gr.at[hl, me], base + j, dp
+    def g_send(hl, i):
+        return remote(
+            kvf.at[hl, i], kvg.at[hl * 4 + mine], gs.at[hl, i], gr.at[hl, mine], base + i, dp
         )
 
     def g_arrive(hl, j):
         return remote(
-            kvf.at[hl, j], kvg.at[hl * 4 + j], gs.at[hl, j], gr.at[hl, j], base + j, dp
+            kvf.at[hl, j], kvg.at[hl * 4 + j], gs.at[hl, j], gr.at[hl, j], base + owner(j, dp), dp
         )
 
     def g_local(hl):
-        return pltpu.make_async_copy(kvf.at[hl, me], kvg.at[hl * 4 + me], gl.at[hl])
+        return pltpu.make_async_copy(kvf.at[hl, me], kvg.at[hl * 4 + mine], gl.at[hl])
 
     def p_send(hl, i):
-        return remote(kvf.at[hl, i], kvp.at[hl, i], ps.at[hl, i], pr.at[hl, i], seq, other)
+        return remote(
+            kvf.at[hl, i], kvp.at[hl, i], ps.at[hl, i], pr.at[hl, i], twin_seq, other
+        )
 
     def x_seq(x):
         return zi * 16 + x * 4 + me
@@ -218,57 +242,57 @@
     def second_arrive(hl, z):
         return remote(dz.at[hl, z], r2.at[hl, z], s2s.at[hl, z], s2r.at[hl, z], z_seq(z), dp)
 
-    def third(j):
-        return remote(s3.at[j], r3.at[me], s3s.at[j], s3r.at[me], base + j, dp)
+    def third(i):
+        return remote(s3.at[i], r3.at[mine], s3s.at[i], s3r.at[mine], base + i, dp)
 
     def third_arrive(j):
-        return remote(s3.at[j], r3.at[j], s3s.at[j], s3r.at[j], base + j, dp)
+        return remote(s3.at[j], r3.at[j], s3s.at[j], s3r.at[j], base + owner(j, dp), dp)
 
     def others(body):
         loop(1, 4, lambda r: body((me + r) % 4))
 
-    def project(hl):
+    def owners(body):
+        loop(1, 4, lambda r: body((mine + r) % 4))
+
+    def project(hl, kv):
         def forward(j):
-            w_arrive(hl, j, 0).wait_recv()
-            w_arrive(hl, j, 1).wait_recv()
-            w_swap(hl, j, core).start()
+            w_arrive(hl, j, kv).wait_recv()
+            w_swap(hl, j, kv, core).start()
 
         loop(0, 4, forward)
 
-        def one(r):
-            j = (me + r) % 4
-            w_local(hl, j, 0).wait()
-            w_local(hl, j, 1).wait()
-            w_swap(hl, j, 1 - core).wait_recv()
-            kv = jnp.dot(xv[...], wf[hl * 4 + j], preferred_element_type=F32)
-            stage[hl * 4 + j] = kv.astype(BF)
-
-            @pl.when(r < 4)
-            def _():
-                kv_send(hl, j).start()
-
-            @pl.when(r == 4)
-            def _():
-                kv_local(hl).start()
-
-        loop(1, 5, one)
-
-    def send_halo(hl):
-        kv_local(hl).wait()
+        def two(pair):
+            halves = []
+            for j in (2 * pair, 2 * pair + 1):
+                w_local(hl, j, kv).wait()
+                w_swap(hl, j, kv, 1 - core).wait_recv()
+                halves.append(wf[hl * 4 + j, :, kv * HD:(kv + 1) * HD])
+            both = jnp.dot(
+                xv[...], jnp.concatenate(halves, axis=1), preferred_element_type=F32
+            ).astype(BF)
+            for k in range(2):
+                stage[kv, hl * 4 + 2 * pair + k] = both[:, k * HD:(k + 1) * HD]
+
+        loop(0, 2, two)
+        owners(lambda j: kv_send(hl, kv, j).start())
+        kv_local(hl, kv).start()
+
+    def send_halo(hl, kv):
+        kv_local(hl, kv).wait()
 
         def go(i):
-            halo(hl, i, 0).start()
-            halo(hl, i, 1).start()
+            halo(hl, kv, i, 0).start()
+            halo(hl, kv, i, 1).start()
 
         go(me)
 
         def one(i):
-            kv_arrive(hl, i).wait_recv()
+            kv_arrive(hl, kv, i).wait_recv()
             go(i)
 
         others(one)
 
-    def attend(hl):
+    def attend(hl, lo, hi):
         rows = lax.broadcasted_iota(jnp.int32, (BLK, BLK), 0)
         columns = lax.broadcasted_iota(jnp.int32, (BLK, BLK), 1)
 
@@ -279,7 +303,7 @@
             top = None
             for w in range(SPAN + 1):
                 scores = lax.dot_general(
-                    kbuf[hl, qi + w, :, :HD], query, NT, preferred_element_type=F32
+                    kbuf[hl, 0, qi + w], query, NT, preferred_element_type=F32
                 )
                 if w == 0:
                     scores = jnp.where(rows > columns, scores, NEG)
@@ -291,7 +315,7 @@
                     here = jnp.where(first + w >= 0, here, NEG)
                 top = here if top is None else jnp.maximum(top, here)
                 dp_ref[w] = lax.dot_general(
-                    kbuf[hl, qi + w, :, HD:], grad, NT, preferred_element_type=F32
+                    kbuf[hl, 1, qi + w], grad, NT, preferred_element_type=F32
                 )
             top = top * EXP_SCALE
             total = jnp.zeros((1, BLK), F32)
@@ -313,8 +337,8 @@
                 dscore = ((e * inverse_scaled) * (dp_ref[w] - mean)).astype(BF)
                 dkv[hl, qi + w, :, :HD] += jnp.dot(dscore, query, preferred_element_type=F32)
                 dkv[hl, qi + w, :, HD:] += jnp.dot(weights, grad, preferred_element_type=F32)
-                att = att + jnp.dot(kvt[hl, qi + w, HD:, :], weights, preferred_element_type=F32)
-                dq = dq + jnp.dot(kvt[hl, qi + w, :HD, :], dscore, preferred_element_type=F32)
+                att = att + jnp.dot(kvt[hl, 1, qi + w], weights, preferred_element_type=F32)
+                dq = dq + jnp.dot(kvt[hl, 0, qi + w], dscore, preferred_element_type=F32)
             obuf[hl, qi, :, :HD] = att.T.astype(BF)
             obuf[hl, qi, :, HD:] = dq.T.astype(BF)
 
@@ -331,7 +355,9 @@
             sbuf[hl, qi] = dkv[hl, qi].astype(BF)
             back(hl, qi, 1).start()
 
-        loop(0, 4, one_block)
+        loop(lo, hi, one_block)
+        if hi < 4:
+            return
 
         def one_back(i):
             sbuf[hl, 4 + i] = dkv[hl, 4 + i].astype(BF)
@@ -383,6 +409,8 @@
                     dwb[hl, xx, 2 * t + zz] = acc[lo:lo + 32].astype(BF)
 
         loop(0, 4, tile)
+
+    def first_stage(hl):
         loop(1, 4, lambda r: first(hl, (xi + r) % 4).start())
 
     def add_x(hl, z):
@@ -409,12 +437,8 @@
         for j in range(4):
             s3[j, :, hl * 256:(hl + 1) * 256] = acc[j * 8:(j + 1) * 8]
 
-    def w_start(hl):
-        def one(j):
-            w_send(hl, j, 0).start()
-            w_send(hl, j, 1).start()
-
-        loop(0, 4, one)
+    def w_start(hl, kv):
+        loop(0, 4, lambda j: w_send(hl, j, kv).start())
 
     def q_start(hl):
         q_local(hl, 0).start()
@@ -424,31 +448,35 @@
             q_send(hl, j, 0).start()
             q_send(hl, j, 1).start()
 
-        others(one)
-
-    def turn(hl, b):
-        dkv[hl, b] = jnp.zeros((BLK, 2 * HD), F32)
-        kvt[hl, b] = kbuf[hl, b].T
+        owners(one)
 
     def ready(hl):
-        loop(SPAN, SPAN + 4, lambda b: turn(hl, b))
-
-        def near(i):
-            halo(hl, i, 0).wait_recv()
-            turn(hl, 4 + i)
-
-        def far(i):
-            halo(hl, i, 1).wait_recv()
-            turn(hl, i)
-
-        loop(0, 4, near)
-        loop(0, 4, far)
+        for kv in range(2):
+            def turn(b):
+                kvt[hl, kv, b] = kbuf[hl, kv, b].T
+
+            def near(i):
+                halo(hl, kv, i, 0).wait_recv()
+                turn(4 + i)
+
+            def far(i):
+                halo(hl, kv, i, 1).wait_recv()
+                turn(i)
+
+            loop(SPAN, SPAN + 4, turn)
+            loop(0, 4, near)
+            loop(0, 4, far)
+
+        def clear(b):
+            dkv[hl, b] = jnp.zeros((BLK, 2 * HD), F32)
+
+        loop(0, 12, clear)
         q_local(hl, 0).wait()
         q_local(hl, 1).wait()
 
-        def two(j):
-            q_arrive(hl, j, 0).wait_recv()
-            q_arrive(hl, j, 1).wait_recv()
+        def two(i):
+            q_arrive(hl, i, 0).wait_recv()
+            q_arrive(hl, i, 1).wait_recv()
 
         others(two)
 
@@ -466,14 +494,13 @@
     for hl in range(2):
         for kv in range(2):
             loop(0, 4, lambda j: w_local(hl, j, kv).start())
-    greet(
+    wait_all = greet(
         [(base + (me + r) % 4, dp) for r in range(1, 4)]
         + [(base + (me + r) % 4, other) for r in range(4)]
         + [(near_next, dp), (far_next, dp), (near_prev, dp), (far_prev, dp)]
         + [(x_seq((xi + r) % 4), dp) for r in range(1, 4)]
         + [(z_seq((zi + r) % n_z), dp) for r in range(1, n_z)]
     )
-    w_start(0)
     x_copy.wait()
 
     def flip(t):
@@ -481,41 +508,59 @@
         xt[pl.ds(at, 256), :] = xv[:, pl.ds(at, 256)].T
 
     loop(0, 8, flip)
-    project(0)
-    others(lambda j: kv_send(0, j).wait_send())
-    w_start(1)
-    send_halo(0)
-    project(1)
+    f_local().start()
+    wait_all()
+    w_start(0, 0)
+    project(0, 0)
+    w_start(0, 1)
+    send_halo(0, 0)
+    project(0, 1)
+    w_start(1, 0)
+    send_halo(0, 1)
+    project(1, 0)
+    w_start(1, 1)
     q_start(0)
+    send_halo(1, 0)
+    project(1, 1)
     q_start(1)
-    send_halo(1)
-    f_local().start()
-    loop(1, 8, lambda t: f_send((me + t % 4) % 4, (dp + t // 4) % 2).start())
+    send_halo(1, 1)
+    f_local().wait()
+    f_pass(0, core).start()
+    loop(1, 4, lambda t: f_send(t).start())
     ready(0)
-    attend(0)
+    attend(0, 0, 4)
     ready(1)
-    attend(1)
+    attend(1, 0, 2)
     finish(0)
-    f_local().wait()
-    loop(1, 8, lambda t: f_arrive((me + t % 4) % 4, (dp + t // 4) % 2).wait_recv())
+
+    def hand_over(t):
+        f_arrive(t).wait_recv()
+        f_pass(t, core).start()
+
+    loop(1, 4, hand_over)
+    attend(1, 2, 4)
+    loop(0, 4, lambda t: f_pass(t, 1 - core).wait_recv())
     product_own(0)
+    product_other(0)
     finish(1)
-    product_other(0)
+    owners(lambda j: g_arrive(0, j).wait_recv())
+    first_stage(0)
     product_own(1)
-    for hl in range(2):
-        g_local(hl).wait()
-        others(lambda j: g_arrive(hl, j).wait_recv())
     product_other(1)
+    first_stage(1)
     second_stage(0)
+    g_local(0).wait()
+    g_local(1).wait()
+    owners(lambda j: g_arrive(1, j).wait_recv())
     loop(0, 8, feature)
     fg_copy = pltpu.make_async_copy(fgv, fg_out, el)
     fg_copy.start()
     second_stage(1)
     third_stage(0)
     third_stage(1)
-    loop(1, 4, lambda r: third((me + r) % 4).start())
-    r3[me] = s3[me]
-    loop(1, 4, lambda r: third_arrive((me + r) % 4).wait_recv())
+    others(lambda i: third(i).start())
+    r3[mine] = s3[me]
+    owners(lambda j: third_arrive(j).wait_recv())
     for j in range(4):
         for hl in range(2):
             for kv in range(2):
@@ -524,37 +569,47 @@
                 dw_out[:, head:head + HD] = r3[j, :, lo:lo + HD]
 
     for hl in range(2):
-        def w_end(j):
-            w_send(hl, j, 0).wait_send()
-            w_send(hl, j, 1).wait_send()
-            w_swap(hl, j, core).wait_send()
-
-        loop(0, 4, w_end)
+        for kv in range(2):
+            def w_end(j):
+                w_send(hl, j, kv).wait_send()
+                w_swap(hl, j, kv, core).wait_send()
+
+            loop(0, 4, w_end)
+            owners(lambda j: kv_send(hl, kv, j).wait_send())
+
+            def halo_end(i):
+                halo(hl, kv, i, 0).wait_send()
+                halo(hl, kv, i, 1).wait_send()
+
+            loop(0, 4, halo_end)
 
         def four_end(i):
             for far in range(2):
-                halo(hl, i, far).wait_send()
                 back(hl, i, far).wait_send()
             p_send(hl, i).wait_send()
 
         loop(0, 4, four_end)
 
-        def three_end(j):
-            if hl == 1:
-                kv_send(hl, j).wait_send()
-            g_send(hl, j).wait_send()
+        def owners_end(j):
             for which in range(2):
                 q_send(hl, j, which).wait_send()
-                o_send(hl, j, which).wait_send()
                 o_arrive(hl, j, which).wait_recv()
 
-        others(three_end)
+        owners(owners_end)
+
+        def others_end(i):
+            g_send(hl, i).wait_send()
+            for which in range(2):
+                o_send(hl, i, which).wait_send()
+
+        others(others_end)
         o_local(hl, 0).wait()
         o_local(hl, 1).wait()
         loop(1, 4, lambda r: first(hl, (xi + r) % 4).wait_send())
         loop(1, n_z, lambda r: second(hl, (zi + r) % n_z).wait_send())
-    loop(1, 8, lambda t: f_send((me + t % 4) % 4, (dp + t // 4) % 2).wait_send())
-    loop(1, 4, lambda r: third((me + r) % 4).wait_send())
+    loop(1, 4, lambda t: f_send(t).wait_send())
+    loop(0, 4, lambda t: f_pass(t, core).wait_send())
+    others(lambda i: third(i).wait_send())
     fg_copy.wait()
 
 
@@ -573,9 +628,9 @@
             pltpu.VMEM((8, 2048, 256), BF),
             pltpu.VMEM((256, 2048), BF),
             pltpu.VMEM((2048, 256), BF),
-            pltpu.VMEM((8, 256, 256), BF),
-            pltpu.VMEM((2, 12, 256, 256), BF),
-            pltpu.VMEM((2, 12, 256, 256), BF),
+            pltpu.VMEM((2, 8, 256, 128), BF),
+            pltpu.VMEM((2, 2, 12, 256, 128), BF),
+            pltpu.VMEM((2, 2, 12, 128, 256), BF),
             pltpu.VMEM((2, 4, 256, 256), BF),
             pltpu.VMEM((9, 256, 256), F32),
             pltpu.VMEM((9, 256, 256), F32),
@@ -595,11 +650,11 @@
             pltpu.VMEM((2, 8, 32, 256), BF),
             pltpu.VMEM((4, 8, 512), F32),
             pltpu.VMEM((4, 8, 512), F32),
-            dma((8, 2)), dma((8, 2)), dma((8, 2)), dma((8,)), dma((8,)), dma,
-            dma((2, 4)), dma((2, 4)), dma((2,)),
-            dma((2, 2, 4)), dma((2, 2, 4)),
+            dma((8, 2)), dma((8, 2)), dma((8, 2)), dma((8, 2)), dma((8, 2)), dma,
+            dma((2, 2, 4)), dma((2, 2, 4)), dma((2, 2)),
+            dma((2, 2, 2, 4)), dma((2, 2, 2, 4)),
             dma((2, 4, 2)), dma((2, 4, 2)), dma((2, 2)),
-            dma((2, 4)), dma((2, 4)), dma,
+            dma((2, 2)), dma((2, 2)), dma, dma((2, 2)), dma((2, 2)),
             dma((2, 4, 2)), dma((2, 4, 2)), dma((2, 2)),
             dma((2, 2, 4)), dma((2, 2, 4)),
             dma((2, 4)), dma((2, 4)), dma((2,)), dma,

time: 184 us -> 162 us (0.88)
  Pallas kernels: 177 us -> 154 us
    pallas_call x1, Pallas kernels: 177 us -> 154 us  [local(): pl.pallas_call(attention_kernel, out_shape=(sds((256, 1024), BF), sds((25...]
where the time goes in v3:
time: 162 us
  Pallas kernels  154 us (95%)
  local copies, waits for them, and re-layouts  6.7 us (4%)
    pallas_call x1, Pallas kernels, local(): pl.pallas_call(attention_kernel, out_shape=(sds((256, 1024), BF), sds((25...  154 us
    unnamed x6, local copies, waits for them, and re-layouts  6.7 us

profile of v3, /device:TPU:1, one launch (start us, length us, event | category | flops | bytes accessed | tf_op | source)
XLA Modules:
  0.0 161.6 jit_solution(18205184144835408442)
XLA Ops:
  0.6 154.3 %attention.1 = (bf16[256,1024]{1,0:T(8,128)(2,1)}, bf16[256,1024]{1,0:T(8,128)(2,1)}, bf16[256,2048]{1,0:T(8,128)(2,1)}, f32[8,2048]{1,0:T(8,128)}) custom-call(bf16[256,2048]{1,0:T(8,128)(2,1)} %bitcast.7, bf16[256,1024]{1,0:T(8,128)(2,1)} %bitcast.8, bf16[1024,2048]{1,0:T(8,128)(2,1)} %w_in.1, bf16[256,1024]{1,0:T(8,128)(2,1)} %bitcast.9), custom_call_target="tpu_custom_call" | custom-call | tf_op jit(solution)/shard_map/attention/pallas_call | solution.py:620
  154.9 0.0 copy-start
  154.9 1.9 %copy.12 = bf16[1,256,1024]{2,1,0:T(8,128)(2,1)} copy(bf16[1,256,1024]{2,1,0:T(8,128)(2,1)} %bitcast.11) | data formatting | bytes 1048576
  156.8 1.9 %copy.13 = bf16[1,256,1024]{2,1,0:T(8,128)(2,1)} copy(bf16[1,256,1024]{2,1,0:T(8,128)(2,1)} %bitcast.10) | data formatting | bytes 1048576
  158.7 2.3 %copy.14 = bf16[1,256,2048]{2,1,0:T(8,128)(2,1)} copy(bf16[1,256,2048]{2,1,0:T(8,128)(2,1)} %bitcast.6) | data formatting | bytes 2097152
  161.0 0.0 copy-done
  161.0 0.6 copy.15
Async XLA Ops:
  154.9 6.1 %copy-start = (f32[8,2048]{1,0:T(8,128)S(1)}, f32[8,2048]{1,0:T(8,128)}, u32[]{:S(2)}) copy-start(f32[8,2048]{1,0:T(8,128)} %get-tuple-element.19) | copy-start | bytes 196612

commit v4 on v3

--- a/solution.py
+++ b/solution.py
@@ -50,7 +50,7 @@
 def attention_kernel(
     x_in, q_in, w_in, up_in,
     att_out, dq_out, fg_out, dw_out,
-    wf, xv, xt, stage, kbuf, kvt, qbuf, s_ref, dp_ref, dkv, sbuf, rbuf, kvf, kvp, kvg, obuf, fgv,
+    wf, pacc, xv, xt, stage, kbuf, kvt, qbuf, s_ref, dp_ref, dkv, sbuf, rbuf, kvf, kvp, kvg, obuf, fgv,
     fv, dwa, dwb, r1, dz, r2, s3, r3,
     wl, ws, wr, wfs, wfr, xl, ks, kr, kl, hs, hr, qs, qr, ql, fs, fr, fl, fps, fpr,
     os_, or_, ol, rs, rr, gs, gr, gl, el,
@@ -72,38 +72,44 @@
     twin_seq = base + owner(mine, other)
     w_seq = base + ((y_hi + (1 - dp) * (1 - core) + dp * core) % 2) * 2 + core
     pair_seq = base + y_hi * 2 + (1 - core)
-    near_next = (seq + 4) % n_seq
-    far_next = (seq + 8) % n_seq
-    near_prev = (seq + n_seq - 4) % n_seq
-    far_prev = (seq + n_seq - 8) % n_seq
+    next_seq = (seq + 4) % n_seq
+    prev_seq = (seq + n_seq - 4) % n_seq
 
     def cols(head_pos, kv):
         return pl.ds(pl.multiple_of(kv * 1024 + head_pos * HD, HD), HD)
 
-    def w_local(hl, j, kv):
+    def w_at(hl, kv, p):
+        return (hl * 2 + kv) * 2 + p
+
+    def half(e):
+        return pl.ds(e * HD, HD)
+
+    def w_local(hl, kv, p, e):
         return pltpu.make_async_copy(
-            w_in.at[:, cols(2 * j + hl, kv)],
-            wf.at[hl * 4 + j, pl.ds(pl.multiple_of(dp * 1024, 1024), 1024), pl.ds(kv * HD, HD)],
-            wl.at[hl * 4 + j, kv],
+            w_in.at[:, cols(2 * (2 * p + e) + hl, kv)],
+            wf.at[w_at(hl, kv, p), pl.ds(pl.multiple_of(dp * 1024, 1024), 1024), half(e)],
+            wl.at[w_at(hl, kv, p), e],
         )
 
     def w_rows(which_dp, which_core):
         return pl.ds(pl.multiple_of(which_dp * 1024 + which_core * 512, 512), 512)
 
-    def w_send(hl, j, kv):
-        return remote(
-            w_in.at[pl.ds(pl.multiple_of(core * 512, 512), 512), cols(2 * j + hl, kv)],
-            wf.at[hl * 4 + j, w_rows(dp, core), pl.ds(kv * HD, HD)],
-            ws.at[hl * 4 + j, kv], wr.at[hl * 4 + j, kv], w_seq, other,
-        )
-
-    def w_arrive(hl, j, kv):
-        part = wf.at[hl * 4 + j, w_rows(other, core), pl.ds(kv * HD, HD)]
-        return remote(part, part, ws.at[hl * 4 + j, kv], wr.at[hl * 4 + j, kv], w_seq, other)
-
-    def w_swap(hl, j, kv, which_core):
-        part = wf.at[hl * 4 + j, w_rows(other, which_core), pl.ds(kv * HD, HD)]
-        return remote(part, part, wfs.at[hl * 4 + j, kv], wfr.at[hl * 4 + j, kv], pair_seq, dp)
+    def w_send(hl, kv, p, e):
+        at = w_at(hl, kv, p)
+        return remote(
+            w_in.at[pl.ds(pl.multiple_of(core * 512, 512), 512), cols(2 * (2 * p + e) + hl, kv)],
+            wf.at[at, w_rows(dp, core), half(e)], ws.at[at, e], wr.at[at, e], w_seq, other,
+        )
+
+    def w_arrive(hl, kv, p, e):
+        at = w_at(hl, kv, p)
+        part = wf.at[at, w_rows(other, core), half(e)]
+        return remote(part, part, ws.at[at, e], wr.at[at, e], w_seq, other)
+
+    def w_swap(hl, kv, p, which_core):
+        at = w_at(hl, kv, p)
+        part = wf.at[at, w_rows(other, which_core), :]
+        return remote(part, part, wfs.at[at], wfr.at[at], pair_seq, dp)
 
     def kv_send(hl, kv, j):
         return remote(
@@ -124,8 +130,8 @@
 
     def halo(hl, kv, i, far):
         return remote(
-            kbuf.at[hl, kv, SPAN + i], kbuf.at[hl, kv, (1 - far) * 4 + i],
-            hs.at[hl, kv, far, i], hr.at[hl, kv, far, i], far_next if far else near_next, dp,
+            kbuf.at[hl, kv, (2 - far) * 4 + i], kbuf.at[hl, kv, (1 - far) * 4 + i],
+            hs.at[hl, kv, far, i], hr.at[hl, kv, far, i], next_seq, dp,
         )
 
     def q_copy(hl, j, which):
@@ -199,21 +205,28 @@
     def back(hl, i, far):
         return remote(
             sbuf.at[hl, (1 - far) * 4 + i], rbuf.at[hl, far, i],
-            rs.at[hl, far, i], rr.at[hl, far, i], far_prev if far else near_prev, dp,
-        )
-
-    def g_send(hl, i):
-        return remote(
-            kvf.at[hl, i], kvg.at[hl * 4 + mine], gs.at[hl, i], gr.at[hl, mine], base + i, dp
-        )
-
-    def g_arrive(hl, j):
-        return remote(
-            kvf.at[hl, j], kvg.at[hl * 4 + j], gs.at[hl, j], gr.at[hl, j], base + owner(j, dp), dp
-        )
-
-    def g_local(hl):
-        return pltpu.make_async_copy(kvf.at[hl, me], kvg.at[hl * 4 + mine], gl.at[hl])
+            rs.at[hl, far, i], rr.at[hl, far, i], prev_seq, dp,
+        )
+
+    def g_slot(hl, kv, j):
+        return kvg.at[w_at(hl, kv, j // 2), :, pl.ds(pl.multiple_of(j % 2 * HD, HD), HD)]
+
+    def g_send(hl, i, kv):
+        return remote(
+            kvf.at[hl, i, :, half(kv)], g_slot(hl, kv, mine),
+            gs.at[hl, i, kv], gr.at[hl, mine, kv], base + i, dp,
+        )
+
+    def g_arrive(hl, j, kv):
+        return remote(
+            kvf.at[hl, j, :, half(kv)], g_slot(hl, kv, j),
+            gs.at[hl, j, kv], gr.at[hl, j, kv], base + owner(j, dp), dp,
+        )
+
+    def g_local(hl, kv):
+        return pltpu.make_async_copy(
+            kvf.at[hl, me, :, half(kv)], g_slot(hl, kv, mine), gl.at[hl, kv]
+        )
 
     def p_send(hl, i):
         return remote(
@@ -254,43 +267,62 @@
     def owners(body):
         loop(1, 4, lambda r: body((mine + r) % 4))
 
-    def project(hl, kv):
-        def forward(j):
-            w_arrive(hl, j, kv).wait_recv()
-            w_swap(hl, j, kv, core).start()
-
-        loop(0, 4, forward)
-
-        def two(pair):
-            halves = []
-            for j in (2 * pair, 2 * pair + 1):
-                w_local(hl, j, kv).wait()
-                w_swap(hl, j, kv, 1 - core).wait_recv()
-                halves.append(wf[hl * 4 + j, :, kv * HD:(kv + 1) * HD])
-            both = jnp.dot(
-                xv[...], jnp.concatenate(halves, axis=1), preferred_element_type=F32
-            ).astype(BF)
-            for k in range(2):
-                stage[kv, hl * 4 + 2 * pair + k] = both[:, k * HD:(k + 1) * HD]
-
-        loop(0, 2, two)
+    def x_cols(which_dp):
+        return xv[:, pl.ds(pl.multiple_of(which_dp * 1024, 1024), 1024)]
+
+    def w_half(hl, kv, p, which_dp):
+        return wf[w_at(hl, kv, p), pl.ds(pl.multiple_of(which_dp * 1024, 1024), 1024), :]
+
+    def project_own(hl, kv):
+        def one(p):
+            w_local(hl, kv, p, 0).wait()
+            w_local(hl, kv, p, 1).wait()
+            pacc[w_at(hl, kv, p)] = jnp.dot(
+                x_cols(dp), w_half(hl, kv, p, dp), preferred_element_type=F32
+            )
+
+        loop(0, 2, one)
+
+    def project(hl, kv, then=None):
+        def forward(p):
+            w_arrive(hl, kv, p, 0).wait_recv()
+            w_arrive(hl, kv, p, 1).wait_recv()
+            w_swap(hl, kv, p, core).start()
+            if then is not None:
+                w_send(*then, p, 0).start()
+                w_send(*then, p, 1).start()
+
+        loop(0, 2, forward)
+
+        def one(p):
+            w_swap(hl, kv, p, 1 - core).wait_recv()
+            both = pacc[w_at(hl, kv, p)] + jnp.dot(
+                x_cols(other), w_half(hl, kv, p, other), preferred_element_type=F32
+            )
+            for e in range(2):
+                stage[kv, hl * 4 + 2 * p + e] = both[:, e * HD:(e + 1) * HD].astype(BF)
+
+        loop(0, 2, one)
         owners(lambda j: kv_send(hl, kv, j).start())
         kv_local(hl, kv).start()
 
     def send_halo(hl, kv):
         kv_local(hl, kv).wait()
 
-        def go(i):
-            halo(hl, kv, i, 0).start()
-            halo(hl, kv, i, 1).start()
-
-        go(me)
+        halo(hl, kv, me, 0).start()
 
         def one(i):
             kv_arrive(hl, kv, i).wait_recv()
-            go(i)
+            halo(hl, kv, i, 0).start()
 
         others(one)
+
+    def relay(hl, kv):
+        def one(i):
+            halo(hl, kv, i, 0).wait_recv()
+            halo(hl, kv, i, 1).start()
+
+        loop(1, 5, lambda r: one((me + r - 1) % 4))
 
     def attend(hl, lo, hi):
         rows = lax.broadcasted_iota(jnp.int32, (BLK, BLK), 0)
@@ -360,7 +392,8 @@
             return
 
         def one_back(i):
-            sbuf[hl, 4 + i] = dkv[hl, 4 + i].astype(BF)
+            back(hl, i, 1).wait_recv()
+            sbuf[hl, 4 + i] = (dkv[hl, 4 + i] + rbuf[hl, 1, i].astype(F32)).astype(BF)
             back(hl, i, 0).start()
 
         loop(0, 4, one_back)
@@ -368,18 +401,19 @@
     def finish(hl):
         def one(i):
             back(hl, i, 0).wait_recv()
-            back(hl, i, 1).wait_recv()
-            whole = dkv[hl, SPAN + i] + rbuf[hl, 0, i].astype(F32) + rbuf[hl, 1, i].astype(F32)
+            whole = dkv[hl, SPAN + i] + rbuf[hl, 0, i].astype(F32)
             kvf[hl, i] = whole.astype(BF)
             p_send(hl, i).start()
 
             @pl.when(i == me)
             def _():
-                g_local(hl).start()
+                g_local(hl, 0).start()
+                g_local(hl, 1).start()
 
             @pl.when(i != me)
             def _():
-                g_send(hl, i).start()
+                g_send(hl, i, 0).start()
+                g_send(hl, i, 1).start()
 
         loop(0, 4, one)
 
@@ -438,7 +472,11 @@
             s3[j, :, hl * 256:(hl + 1) * 256] = acc[j * 8:(j + 1) * 8]
 
     def w_start(hl, kv):
-        loop(0, 4, lambda j: w_send(hl, j, kv).start())
+        def one(p):
+            w_send(hl, kv, p, 0).start()
+            w_send(hl, kv, p, 1).start()
+
+        loop(0, 2, one)
 
     def q_start(hl):
         q_local(hl, 0).start()
@@ -455,16 +493,11 @@
             def turn(b):
                 kvt[hl, kv, b] = kbuf[hl, kv, b].T
 
-            def near(i):
-                halo(hl, kv, i, 0).wait_recv()
-                turn(4 + i)
-
             def far(i):
                 halo(hl, kv, i, 1).wait_recv()
                 turn(i)
 
-            loop(SPAN, SPAN + 4, turn)
-            loop(0, 4, near)
+            loop(4, SPAN + 4, turn)
             loop(0, 4, far)
 
         def clear(b):
@@ -493,11 +526,12 @@
     x_copy.start()
     for hl in range(2):
         for kv in range(2):
-            loop(0, 4, lambda j: w_local(hl, j, kv).start())
+            for e in range(2):
+                loop(0, 2, lambda p: w_local(hl, kv, p, e).start())
     wait_all = greet(
         [(base + (me + r) % 4, dp) for r in range(1, 4)]
         + [(base + (me + r) % 4, other) for r in range(4)]
-        + [(near_next, dp), (far_next, dp), (near_prev, dp), (far_prev, dp)]
+        + [(next_seq, dp), (prev_seq, dp)]
         + [(x_seq((xi + r) % 4), dp) for r in range(1, 4)]
         + [(z_seq((zi + r) % n_z), dp) for r in range(1, n_z)]
     )
@@ -509,49 +543,56 @@
 
     loop(0, 8, flip)
     f_local().start()
+    for hl in range(2):
+        for kv in range(2):
+            project_own(hl, kv)
     wait_all()
     w_start(0, 0)
-    project(0, 0)
-    w_start(0, 1)
+    project(0, 0, (0, 1))
     send_halo(0, 0)
-    project(0, 1)
-    w_start(1, 0)
+    project(0, 1, (1, 0))
+    q_start(0)
+    relay(0, 0)
     send_halo(0, 1)
-    project(1, 0)
-    w_start(1, 1)
-    q_start(0)
+    project(1, 0, (1, 1))
+    relay(0, 1)
     send_halo(1, 0)
+    ready(0)
+    attend(0, 0, 1)
     project(1, 1)
     q_start(1)
+    relay(1, 0)
+    attend(0, 1, 2)
     send_halo(1, 1)
+    attend(0, 2, 3)
+    relay(1, 1)
     f_local().wait()
     f_pass(0, core).start()
     loop(1, 4, lambda t: f_send(t).start())
-    ready(0)
-    attend(0, 0, 4)
+    attend(0, 3, 4)
     ready(1)
     attend(1, 0, 2)
     finish(0)
+    attend(1, 2, 4)
+    finish(1)
 
     def hand_over(t):
         f_arrive(t).wait_recv()
         f_pass(t, core).start()
 
     loop(1, 4, hand_over)
-    attend(1, 2, 4)
     loop(0, 4, lambda t: f_pass(t, 1 - core).wait_recv())
     product_own(0)
     product_other(0)
-    finish(1)
-    owners(lambda j: g_arrive(0, j).wait_recv())
     first_stage(0)
     product_own(1)
     product_other(1)
     first_stage(1)
     second_stage(0)
-    g_local(0).wait()
-    g_local(1).wait()
-    owners(lambda j: g_arrive(1, j).wait_recv())
+    for hl in range(2):
+        for kv in range(2):
+            g_local(hl, kv).wait()
+            owners(lambda j: g_arrive(hl, j, kv).wait_recv())
     loop(0, 8, feature)
     fg_copy = pltpu.make_async_copy(fgv, fg_out, el)
     fg_copy.start()
@@ -570,11 +611,12 @@
 
     for hl in range(2):
         for kv in range(2):
-            def w_end(j):
-                w_send(hl, j, kv).wait_send()
-                w_swap(hl, j, kv, core).wait_send()
-
-            loop(0, 4, w_end)
+            def w_end(p):
+                w_send(hl, kv, p, 0).wait_send()
+                w_send(hl, kv, p, 1).wait_send()
+                w_swap(hl, kv, p, core).wait_send()
+
+            loop(0, 2, w_end)
             owners(lambda j: kv_send(hl, kv, j).wait_send())
 
             def halo_end(i):
@@ -598,8 +640,8 @@
         owners(owners_end)
 
         def others_end(i):
-            g_send(hl, i).wait_send()
             for which in range(2):
+                g_send(hl, i, which).wait_send()
                 o_send(hl, i, which).wait_send()
 
         others(others_end)
@@ -626,6 +668,7 @@
         out_specs=(anywhere, anywhere, anywhere, pl.BlockSpec(memory_space=pltpu.VMEM)),
         scratch_shapes=[
             pltpu.VMEM((8, 2048, 256), BF),
+            pltpu.VMEM((8, 256, 256), F32),
             pltpu.VMEM((256, 2048), BF),
             pltpu.VMEM((2048, 256), BF),
             pltpu.VMEM((2, 8, 256, 128), BF),
@@ -650,14 +693,14 @@
             pltpu.VMEM((2, 8, 32, 256), BF),
             pltpu.VMEM((4, 8, 512), F32),
             pltpu.VMEM((4, 8, 512), F32),
-            dma((8, 2)), dma((8, 2)), dma((8, 2)), dma((8, 2)), dma((8, 2)), dma,
+            dma((8, 2)), dma((8, 2)), dma((8, 2)), dma((8,)), dma((8,)), dma,
             dma((2, 2, 4)), dma((2, 2, 4)), dma((2, 2)),
             dma((2, 2, 2, 4)), dma((2, 2, 2, 4)),
             dma((2, 4, 2)), dma((2, 4, 2)), dma((2, 2)),
             dma((2, 2)), dma((2, 2)), dma, dma((2, 2)), dma((2, 2)),
             dma((2, 4, 2)), dma((2, 4, 2)), dma((2, 2)),
             dma((2, 2, 4)), dma((2, 2, 4)),
-            dma((2, 4)), dma((2, 4)), dma((2,)), dma,
+            dma((2, 4, 2)), dma((2, 4, 2)), dma((2, 2)), dma,
             dma((2, 4)), dma((2, 4)),
             dma((2, 4)), dma((2, 4)), dma((2, 8)), dma((2, 8)), dma((4,)), dma((4,)),
         ],

time: 162 us -> 160 us (0.988)
  Pallas kernels: 154 us -> 152 us
    pallas_call x1, Pallas kernels: 154 us -> 152 us  [local(): pl.pallas_call(attention_kernel, out_shape=(sds((256, 1024), BF), sds((25...]
where the time goes in v4:
time: 160 us
  Pallas kernels  152 us (95%)
  local copies, waits for them, and re-layouts  6.7 us (4%)
    pallas_call x1, Pallas kernels, local(): pl.pallas_call(attention_kernel, out_shape=(sds((256, 1024), BF), sds((25...  152 us
    unnamed x6, local copies, waits for them, and re-layouts  6.7 us

profile of v4, /device:TPU:1, one launch (start us, length us, event | category | flops | bytes accessed | tf_op | source)
XLA Modules:
  0.0 159.8 jit_solution(15186699816281393543)
XLA Ops:
  0.6 152.4 %attention.1 = (bf16[256,1024]{1,0:T(8,128)(2,1)}, bf16[256,1024]{1,0:T(8,128)(2,1)}, bf16[256,2048]{1,0:T(8,128)(2,1)}, f32[8,2048]{1,0:T(8,128)}) custom-call(bf16[256,2048]{1,0:T(8,128)(2,1)} %bitcast.7, bf16[256,1024]{1,0:T(8,128)(2,1)} %bitcast.8, bf16[1024,2048]{1,0:T(8,128)(2,1)} %w_in.1, bf16[256,1024]{1,0:T(8,128)(2,1)} %bitcast.9), custom_call_target="tpu_custom_call" | custom-call | tf_op jit(solution)/shard_map/attention/pallas_call | solution.py:662
  153.1 0.0 copy-start
  153.1 1.9 %copy.12 = bf16[1,256,1024]{2,1,0:T(8,128)(2,1)} copy(bf16[1,256,1024]{2,1,0:T(8,128)(2,1)} %bitcast.11) | data formatting | bytes 1048576
  155.0 1.9 %copy.13 = bf16[1,256,1024]{2,1,0:T(8,128)(2,1)} copy(bf16[1,256,1024]{2,1,0:T(8,128)(2,1)} %bitcast.10) | data formatting | bytes 1048576
  156.8 2.3 %copy.14 = bf16[1,256,2048]{2,1,0:T(8,128)(2,1)} copy(bf16[1,256,2048]{2,1,0:T(8,128)(2,1)} %bitcast.6) | data formatting | bytes 2097152
  159.1 0.0 copy-done
  159.1 0.6 copy.15
Async XLA Ops:
  153.1 6.1 %copy-start = (f32[8,2048]{1,0:T(8,128)S(1)}, f32[8,2048]{1,0:T(8,128)}, u32[]{:S(2)}) copy-start(f32[8,2048]{1,0:T(8,128)} %get-tuple-element.19) | copy-start | bytes 196612
